TPU v7x, 128 devices: a whole 4x4x4 slice. The times are simulated.
128 devices in a mesh: bead: 2 (over core), space: 64 (over z, y, x).
Axes of the slice: x: 4, y: 4, z: 4, core: 2. Of those that a mesh axis runs over, the one named last changes fastest.
Arguments:
- positions: float32 [32, 3, 65536], P('bead', None, 'space'), may hold values from -6 to 6
- momenta: float32 [32, 3, 65536], P('bead', None, 'space'), may hold values from -6 to 6
- thermostat: float32 [32, 8, 3, 65536], P('bead', None, None, 'space'), may hold values from -6 to 6
- white_noise: float32 [32, 9, 3, 65536], P('bead', None, None, 'space'), may hold values from -6 to 6
- drift_matrix: float32 [32, 9, 9], P('bead'), may hold values from -2 to 2
- noise_matrix: float32 [32, 9, 9], P('bead'), may hold values from -2 to 2
- leave_up: int32 [512], P('space'), may hold values from 0 to 1023, as said below
- leave_down: int32 [512], P('space'), may hold values from 0 to 1023, as said below
- ghost_up: int32 [32768], P('space'), may hold values from 0 to 1023, as said below
- ghost_down: int32 [32768], P('space'), may hold values from 0 to 1023, as said below
- neighbours: int32 [32, 65536], P(None, 'space'), may hold values from 0 to 2047, as said below
Outputs:
- moved_positions: float32 [32, 3, 65536], P('bead', None, 'space')
- moved_momenta: float32 [32, 3, 65536], P('bead', None, 'space')
- moved_thermostat: float32 [32, 8, 3, 65536], P('bead', None, None, 'space')
Inputs may be any that keep to these rules, and one draw needn't show every extreme that they name: Within one slab the 8 rows of leave_up and the 8 rows of leave_down are all distinct; together they are a small share of the slab. Within one slab the rows of leave_down are distinct and none of them is in leave_up. Within one slab the rows of ghost_up are distinct, and together with ghost_down they name every row of the slab once. Within one slab the rows of ghost_down are distinct and none of them is in ghost_up. `neighbours`: an entry equal to the atom's own local row is an empty slot, contributing nothing; in each slab some atom uses all 32 slots.
All inputs are finite; a program needn't handle non-finite values.
Results may differ from a plain program's by a relative error of at most 0.000086.
Values sent between devices are 32-bit elements; how exact they have to be, the bound alone decides.
No kernel may reach another device: no remote copies, remote signals or barrier semaphores. Data moves between devices by JAX's collectives and lax.ppermute only.
A program may use at most 256 MiB of HBM per device.

v0:
```python
import math

import jax
import jax.numpy as jnp
from jax import lax
from jax.sharding import PartitionSpec as P

BEADS = 32


cycle_rate = 0.8
kick_scale = 0.2
core_width = 4.0


def shifted(array, axis, by):
    devices = lax.axis_size(axis)
    return lax.ppermute(array, axis, [(i, (i + by) % devices) for i in range(devices)])


def mode_basis(beads):
    modes = jnp.arange(beads, dtype=jnp.float32)[:, None]
    sites = jnp.arange(beads, dtype=jnp.float32)[None, :]
    angles = 2.0 * math.pi * modes * sites / beads
    cosine = math.sqrt(2.0 / beads) * jnp.cos(angles)
    sine = math.sqrt(2.0 / beads) * jnp.sin(angles)
    edge = jnp.cos(angles) / math.sqrt(beads)
    centre = jnp.full_like(angles, 1.0 / math.sqrt(beads))
    middle = beads // 2
    return jnp.where(
        modes == 0,
        centre,
        jnp.where(modes < middle, cosine, jnp.where(modes == middle, edge, sine)),
    )


def cycle_tables(beads):
    frequency = 2.0 * cycle_rate * jnp.sin(math.pi * jnp.arange(beads, dtype=jnp.float32) / beads)
    nonzero = jnp.where(frequency > 0, frequency, 1.0)
    sine_ratio = jnp.where(frequency > 0, jnp.sin(frequency) / nonzero, 1.0)
    return (jnp.cos(frequency), sine_ratio, frequency * jnp.sin(frequency))


def pair_forces(own, gathered):
    offset = own[..., :, None, :] - gathered
    weight = jnp.exp(-jnp.sum(offset * offset, axis=-3) / (2.0 * core_width))
    return jnp.sum(offset * weight[..., None, :, :], axis=-2)


def per_device(
    positions,
    momenta,
    thermostat,
    white_noise,
    drift_matrix,
    noise_matrix,
    leave_up,
    leave_down,
    ghost_up,
    ghost_down,
    neighbours,
):
    highest = lax.Precision.HIGHEST
    local_beads = positions.shape[0]
    slab_rows = positions.shape[2]
    first_bead = lax.axis_index("bead") * local_beads
    basis = mode_basis(BEADS)
    cosine, sine_ratio, stiffness = cycle_tables(BEADS)

    def transform(values, matrix):
        picked = matrix
        picked = lax.dynamic_slice_in_dim(picked, first_bead, local_beads, 1)
        return lax.psum_scatter(
            jnp.einsum("ob,bcn->ocn", picked, values, precision=highest),
            "bead",
            scatter_dimension=0,
            tiled=True,
        )

    phase = jnp.concatenate([positions, momenta], axis=1)
    in_modes = transform(phase, basis)
    mode_pos = in_modes[:, :3]
    mode_mom = in_modes[:, 3:]
    extended = jnp.concatenate([mode_mom[:, None], thermostat], axis=1)
    evolved = jnp.einsum("kij,kjcn->kicn", drift_matrix, extended, precision=highest) + jnp.einsum(
        "kij,kjcn->kicn", noise_matrix, white_noise, precision=highest
    )
    own_cos = lax.dynamic_slice_in_dim(cosine, first_bead, local_beads)[:, None, None]
    own_ratio = lax.dynamic_slice_in_dim(sine_ratio, first_bead, local_beads)[:, None, None]
    own_stiff = lax.dynamic_slice_in_dim(stiffness, first_bead, local_beads)[:, None, None]
    kicked = evolved[:, 0]
    free_pos = own_cos * mode_pos + own_ratio * kicked
    free_mom = own_cos * kicked - own_stiff * mode_pos
    back_beads = transform(jnp.concatenate([free_pos, free_mom], axis=1), basis.T)
    new_aux = evolved[:, 1:]
    stacked = jnp.concatenate([back_beads, new_aux.reshape(local_beads, -1, slab_rows)], axis=1)
    from_below = shifted(stacked[:, :, leave_up], "space", 1)
    from_above = shifted(stacked[:, :, leave_down], "space", -1)
    stacked = stacked.at[:, :, leave_up].set(from_above).at[:, :, leave_down].set(from_below)
    moved_pos = stacked[:, :3]
    slab_mom = stacked[:, 3:6]
    moved_aux = stacked[:, 6:].reshape(thermostat.shape)
    lower_ghosts = shifted(moved_pos[:, :, ghost_up], "space", 1)
    upper_ghosts = shifted(moved_pos[:, :, ghost_down], "space", -1)
    slab_table = jnp.concatenate([moved_pos, lower_ghosts, upper_ghosts], axis=2)
    gathered = slab_table[:, :, neighbours]
    forces = pair_forces(moved_pos, gathered)
    return (moved_pos, slab_mom + kick_scale * forces, moved_aux)


def solution(mesh):
    in_specs = (
        P("bead", None, "space"),
        P("bead", None, "space"),
        P("bead", None, None, "space"),
        P("bead", None, None, "space"),
        P("bead", None, None),
        P("bead", None, None),
        P("space"),
        P("space"),
        P("space"),
        P("space"),
        P(None, "space"),
    )
    out_specs = (P("bead", None, "space"), P("bead", None, "space"), P("bead", None, None, "space"))
    return jax.shard_map(
        per_device, mesh=mesh, in_specs=in_specs, out_specs=out_specs, check_vma=False
    )
```

profile of v0, /device:TPU:0, one launch (start us, length us, event | category | flops | bytes accessed | tf_op | source)
XLA Modules:
  0.0 663.8 jit_solution(12804816638501555771)
XLA Ops:
  7.4 2.8 fusion.6
  10.8 6.1 fusion.4
  16.9 7.3 %reduce-scatter.3.cloned.1.call-done = f32[16,6,1024]{2,0,1:T(8,128)} async-done(((f32[32,6,1024]{2,0,1:T(8,128)}), f32[16,6,1024]{2,0,1:T(8,128)}) %reduce-scatter.3.cloned.1.call-update) | async-done | bytes 393232 | tf_op jit(solution)/shard_map/reduce_scatter | solution.py:73
  25.5 3.4 fusion
  33.1 12.0 %reduce-scatter.5.cloned.1.call-done = f32[16,6,1024]{2,0,1:T(8,128)} async-done(((f32[32,6,1024]{2,0,1:T(8,128)}), f32[16,6,1024]{2,0,1:T(8,128)}) %reduce-scatter.5.cloned.1.call-update) | async-done | bytes 393232 | tf_op jit(solution)/shard_map/reduce_scatter | solution.py:73
  47.6 7.5 %copy.147 = f32[16,30,1024]{1,0,2:T(8,128)} copy(f32[16,30,1024]{2,0,1:T(8,128)} %pad_maximum_fusion.1) | data formatting | bytes 3932160 | tf_op jit(solution)/shard_map/concatenate | solution.py:96
  55.1 3.9 gather_fusion
  59.0 7.5 %collective-permute-start = (f32[16,30,8]{1,0,2:T(8,128)S(1)}, f32[16,30,8]{1,0,2:T(8,128)S(1)}, u32[]{:S(2)}, u32[]{:S(2)}) collective-permute-start(f32[16,30,8]{1,0,2:T(8,128)S(1)} %bitcast.43), channel_id=1, source_target_pairs={{0,63},{1,0},{2,1},{3,2},{4,3},{5,4},{6,5},{7,6},{8,7},{9,8},{10,9... | collective-permute-start | bytes 46088 | tf_op jit(solution)/shard_map/ppermute | solution.py:18
  66.5 3.9 gather_fusion.1
  72.7 7.6 %collective-permute-done.1 = f32[16,30,8]{1,0,2:T(8,128)S(1)} collective-permute-done((f32[16,30,8]{1,0,2:T(8,128)S(1)}, f32[16,30,8]{1,0,2:T(8,128)S(1)}, u32[]{:S(2)}, u32[]{:S(2)}) %collective-permute-start.1) | collective-permute-done | bytes 15392 | tf_op jit(solution)/shard_map/ppermute | solution.py:18
  82.3 6.3 gather_fusion.2
  88.6 2.9 copy.150
  91.6 6.3 gather_fusion.3
  97.9 2.9 copy.151
  100.7 7.7 %collective-permute-start.3 = (f32[16,3,512]{2,0,1:T(8,128)S(1)}, f32[16,3,512]{2,0,1:T(8,128)S(1)}, u32[]{:S(2)}, u32[]{:S(2)}) collective-permute-start(f32[16,3,512]{2,0,1:T(8,128)S(1)} %copy.151), channel_id=1, source_target_pairs={{0,63},{1,0},{2,1},{3,2},{4,3},{5,4},{6,5},{7,6},{8,7},{9,8},{10,9... | collective-permute-start | bytes 294920 | tf_op jit(solution)/shard_map/ppermute | solution.py:18
  108.5 8.9 %copy.149 = f32[16,3,1024]{0,1,2:T(4,128)} copy(f32[16,3,1024]{1,0,2:T(8,128)} %bitcast.35) | data formatting | bytes 393216 | tf_op jit(solution)/shard_map/slice | solution.py:100
  117.4 8.8 %slice.44 = f32[16,24,1024]{1,0,2:T(8,128)} slice(f32[16,30,1024]{1,0,2:T(8,128)} %scatter_fusion.1), slice={[0:16], [6:30], [0:1024]} | slice | bytes 3145728 | tf_op jit(solution)/shard_map/slice | solution.py:102
  126.2 5.9 copy.159
  132.1 5.5 copy.158
  139.7 3.5 copy.152
  143.3 3.4 copy.153
  146.7 14.0 %pad_maximum_fusion = f32[16,3,2048]{1,0,2:T(8,128)} fusion(f32[16,3,512]{1,0,2:T(8,128)} %copy.153, f32[16,3,512]{1,0,2:T(8,128)} %copy.152, f32[16,3,1024]{1,0,2:T(8,128)} %bitcast.37), kind=kLoop, calls=%fused_computation.9 | loop fusion | flops 196608 | bytes 786432 | tf_op jit(solution)/shard_map/concatenate | solution.py:105
  160.7 15.7 %copy.154 = f32[16,3,2048]{0,1,2:T(4,128)} copy(f32[16,3,2048]{1,0,2:T(8,128)} %pad_maximum_fusion) | data formatting | bytes 786432 | tf_op jit(solution)/shard_map/concatenate | solution.py:105
  176.4 238.2 %gather_fusion.4 = f32[32768,16,3]{1,2,0:T(4,128)} fusion(f32[16,3,2048]{0,1,2:T(4,128)} %copy.154, s32[32768]{0:T(1024)S(1)} %broadcast_clamp_fusion), kind=kCustom, calls=%fused_computation.4 | custom fusion | bytes 12713984 | tf_op jit(solution)/shard_map/gather | solution.py:106
  414.6 163.1 %multiply_reduce_fusion.1 = f32[16,32,1024]{0,2,1:T(8,128)} fusion(f32[16,3,32,1024]{0,1,3,2:T(4,128)} %bitcast.15, f32[16,3,1024]{0,1,2:T(4,128)} %copy.149), kind=kLoop, calls=%fused_computation.8 | loop fusion | flops 4194304 | bytes 8585216 | tf_op jit(solution)/shard_map/reduce_sum | solution.py:46
  577.7 11.1 %copy.155 = f32[16,32,1024]{2,1,0:T(8,128)} copy(f32[16,32,1024]{0,2,1:T(8,128)} %multiply_reduce_fusion.1) | data formatting | bytes 4194304 | tf_op jit(solution)/shard_map/reduce_sum | solution.py:46
  588.7 3.3 multiply_exponential_fusion
  592.0 9.9 %copy.156 = f32[16,32,1024]{0,2,1:T(8,128)} copy(f32[16,32,1024]{2,1,0:T(8,128)} %multiply_exponential_fusion) | data formatting | bytes 4194304 | tf_op jit(solution)/shard_map/exp | solution.py:46
  601.9 28.8 %multiply_reduce_fusion = f32[16,3,1024]{0,1,2:T(4,128)} fusion(f32[16,3,32,1024]{0,1,3,2:T(4,128)} %bitcast.15, f32[16,32,1024]{0,2,1:T(8,128)} %copy.156, f32[16,3,1024]{0,1,2:T(4,128)} %copy.149), kind=kLoop, calls=%fused_computation.7 | loop fusion | flops 4669440 | bytes 8781824 | tf_op jit(solution)/shard_map/reduce_sum | solution.py:47
  630.6 8.6 %copy.157 = f32[16,3,1024]{1,0,2:T(8,128)} copy(f32[16,3,1024]{0,1,2:T(4,128)} %multiply_reduce_fusion) | data formatting | bytes 393216 | tf_op jit(solution)/shard_map/reduce_sum | solution.py:47
  639.3 11.4 %slice_add_fusion = f32[16,3,1024]{1,0,2:T(8,128)} fusion(f32[16,30,1024]{1,0,2:T(8,128)} %scatter_fusion.1, f32[16,3,1024]{1,0,2:T(8,128)} %copy.157), kind=kLoop, calls=%fused_computation.10 | loop fusion | flops 98304 | bytes 589824 | tf_op jit(solution)/shard_map/add | solution.py:108
  650.6 5.9 copy.160
  (62 shorter events, 14.8 us)
Async XLA Ops:
  7.2 3.6 copy-start
  7.2 17.0 %reduce-scatter.3.cloned.1.call-start = ((), (), s32[]{:S(2)}) async-start(), calls=%async_computation.2 | async-start | bytes 1179648 | tf_op jit(solution)/shard_map/reduce_scatter | solution.py:73
  10.2 15.3 %copy-start.3 = (f32[16,8,3,1024]{3,1,2,0:T(8,128)S(1)}, f32[16,8,3,1024]{3,1,2,0:T(8,128)}, u32[]{:S(2)}) copy-start(f32[16,8,3,1024]{3,1,2,0:T(8,128)} %param.13) | copy-start | bytes 4718596
  10.2 15.3 %copy-start.5 = (f32[16,9,9]{2,0,1:T(8,128)S(1)}, f32[16,9,9]{2,0,1:T(8,128)}, u32[]{:S(2)}) copy-start(f32[16,9,9]{2,0,1:T(8,128)} %param.15) | copy-start | bytes 15556
  10.2 34.9 %reduce-scatter.5.cloned.1.call-start = ((), (), s32[]{:S(2)}) async-start(), calls=%async_computation.3 | async-start | bytes 1179648 | tf_op jit(solution)/shard_map/reduce_scatter | solution.py:73
  24.2 4.8 copy-start.2
  29.0 2.0 copy-start.4
  29.0 3.9 copy-start.9
  29.0 3.9 copy-start.10
  29.0 3.9 copy-start.7
  29.0 3.9 copy-start.8
  29.0 3.9 copy-start.6
  59.0 11.7 %collective-permute-start = (f32[16,30,8]{1,0,2:T(8,128)S(1)}, f32[16,30,8]{1,0,2:T(8,128)S(1)}, u32[]{:S(2)}, u32[]{:S(2)}) collective-permute-start(f32[16,30,8]{1,0,2:T(8,128)S(1)} %bitcast.43), channel_id=1, source_target_pairs={{0,63},{1,0},{2,1},{3,2},{4,3},{5,4},{6,5},{7,6},{8,7},{9,8},{10,9... | collective-permute-start | bytes 46088 | tf_op jit(solution)/shard_map/ppermute | solution.py:18
  70.4 9.9 %collective-permute-start.1 = (f32[16,30,8]{1,0,2:T(8,128)S(1)}, f32[16,30,8]{1,0,2:T(8,128)S(1)}, u32[]{:S(2)}, u32[]{:S(2)}) collective-permute-start(f32[16,30,8]{1,0,2:T(8,128)S(1)} %bitcast.42), channel_id=1, source_target_pairs={{0,1},{1,2},{2,3},{3,4},{4,5},{5,6},{6,7},{7,8},{8,9},{9,10},{10,1... | collective-permute-start | bytes 46088 | tf_op jit(solution)/shard_map/ppermute | solution.py:18
  91.5 48.2 %collective-permute-start.2 = (f32[16,3,512]{2,0,1:T(8,128)S(1)}, f32[16,3,512]{2,0,1:T(8,128)S(1)}, u32[]{:S(2)}, u32[]{:S(2)}) collective-permute-start(f32[16,3,512]{2,0,1:T(8,128)S(1)} %copy.150), channel_id=1, source_target_pairs={{0,1},{1,2},{2,3},{3,4},{4,5},{5,6},{6,7},{7,8},{8,9},{9,10},{10,1... | collective-permute-start | bytes 294920 | tf_op jit(solution)/shard_map/ppermute | solution.py:18
  100.7 42.5 %collective-permute-start.3 = (f32[16,3,512]{2,0,1:T(8,128)S(1)}, f32[16,3,512]{2,0,1:T(8,128)S(1)}, u32[]{:S(2)}, u32[]{:S(2)}) collective-permute-start(f32[16,3,512]{2,0,1:T(8,128)S(1)} %copy.151), channel_id=1, source_target_pairs={{0,63},{1,0},{2,1},{3,2},{4,3},{5,4},{6,5},{7,6},{8,7},{9,8},{10,9... | collective-permute-start | bytes 294920 | tf_op jit(solution)/shard_map/ppermute | solution.py:18
  639.3 17.3 %copy-start.1 = (f32[16,9,3,1024]{3,0,2,1:T(8,128)S(1)}, f32[16,9,3,1024]{3,0,2,1:T(8,128)}, u32[]{:S(2)}) copy-start(f32[16,9,3,1024]{3,0,2,1:T(8,128)} %param.14) | copy-start | bytes 5308420
Sparse Core Ops, SparseCore 0:
  10.9 13.2 reduce-scatter.2
  33.0 12.1 reduce-scatter.4
where the time goes:
time: 674 us; the launch traced here: 664 us
  local copies, waits for them, and re-layouts  367 us (54%)
  other arithmetic  225 us (33%)
  waiting for transfers between devices  27 us (4%)
  starting transfers between devices  15.6 us (2%)
  between operations  14.8 us (2%)
  matrix products  14 us (2%)
    gather x1, local copies, waits for them, and re-layouts, per_device(): gathered = slab_table[:, :, neighbours]  238 us
    reduce_sum x1, other arithmetic, pair_forces(): weight = jnp.exp(-jnp.sum(offset * offset, axis=-3) / (2.0 * core_width))  163 us
    reduce_sum x1, other arithmetic, pair_forces(): return jnp.sum(offset * weight[..., None, :, :], axis=-2)  28.8 us
    reduce_scatter x2, waiting for transfers between devices, transform(): lax.psum_scatter(jnp.einsum('ob,bcn->ocn', picked, values, precision=high...  19.3 us
    concatenate x1, local copies, waits for them, and re-layouts, per_device(): jnp.concatenate([moved_pos, lower_ghosts, upper_ghosts], axis=2)  15.7 us
    ppermute x4, starting transfers between devices, shifted(): lax.ppermute(array, axis, [(i, (i + by) % devices) for i in range(devices)])  15.5 us
    slice x2, local copies, waits for them, and re-layouts, per_device(): moved_aux = stacked[:, 6:].reshape(thermostat.shape)  14.4 us
    concatenate x1, other arithmetic, per_device(): jnp.concatenate([moved_pos, lower_ghosts, upper_ghosts], axis=2)  14 us
  transfers between devices with their start and end apart: 6, of which 3 were waited for; matrix products, arithmetic and copies ran while one was open for 9% of the time, Pallas kernels for 0%

commit v1 on v0

v1 whole, which is shorter than its diff:
```python
import functools
import math

import jax
import jax.numpy as jnp
import numpy as np
from jax import lax
from jax.experimental import pallas as pl
from jax.experimental.pallas import tpu as pltpu
from jax.sharding import PartitionSpec as P


BEADS = 32
HALF = 16
ATOMS = 1024
TILES = 8
SLOTS = 32
GHOST_TILES = 4
LANES = 128
FAST = 3
CHUNK = 8

cycle_rate = 0.8
kick_scale = 0.2
core_width = 4.0

F32 = jnp.float32
I32 = jnp.int32
VMEM = pl.BlockSpec(memory_space=pltpu.VMEM)
SMEM = pl.BlockSpec(memory_space=pltpu.SMEM)
ANY = pl.BlockSpec(memory_space=pl.ANY)
HBM = pl.BlockSpec(memory_space=pltpu.HBM)
HIGHEST = lax.Precision.HIGHEST


def constants():
    k = np.arange(BEADS)[:, None].astype(np.float64)
    b = np.arange(BEADS)[None, :].astype(np.float64)
    angle = 2.0 * math.pi * ((k * b) % BEADS) / BEADS
    scale = math.sqrt(2.0 / BEADS)
    basis = np.where(k < BEADS // 2, scale * np.cos(angle), scale * np.sin(angle))
    basis = np.where(k == 0, 1.0 / math.sqrt(BEADS), basis)
    basis = np.where(k == BEADS // 2, np.cos(math.pi * b) / math.sqrt(BEADS), basis)
    w = 2.0 * cycle_rate * np.sin(math.pi * np.arange(BEADS) / BEADS)
    ratio = np.where(w > 0, np.sin(w) / np.where(w > 0, w, 1.0), 1.0)
    columns = np.stack([np.cos(w), ratio, w * np.sin(w)], axis=1)
    forward, backward, tables = [], [], []
    for core in range(2):
        order = np.roll(np.arange(BEADS), -HALF * core)
        forward.append(basis[order][:, order])
        backward.append(basis[order][:, order[:HALF]].T)
        tables.append(np.pad(columns[order], ((0, 0), (0, 5))))
    tables = [np.pad(x, ((0, 0), (0, BEADS - 8))) for x in tables]
    parts = [np.concatenate(x, axis=0) for x in zip(forward, backward, tables)]
    return np.stack(parts).astype(np.float32)


CONSTANTS = constants()


def call(body, outs, args, specs=None, out_specs=None, scratch=(), flops=0, nbytes=0, limit=24, alias=None):
    return pl.pallas_call(
        body,
        out_shape=outs,
        in_specs=specs or [VMEM] * len(args),
        out_specs=out_specs or [VMEM] * len(outs),
        scratch_shapes=scratch,
        input_output_aliases=alias or {},
        compiler_params=pltpu.CompilerParams(vmem_limit_bytes=limit << 20),
        cost_estimate=pl.CostEstimate(flops=flops, bytes_accessed=nbytes, transcendentals=0),
    )(*args)


def struct(*shape, dtype=F32):
    return jax.ShapeDtypeStruct(shape, dtype)


def shifted(array, axis, by):
    devices = lax.axis_size(axis)
    return lax.ppermute(array, axis, [(i, (i + by) % devices) for i in range(devices)])


def take(values, lanes):
    return lax.gather(
        values,
        lanes[..., None],
        lax.GatherDimensionNumbers(
            offset_dims=(),
            collapsed_slice_dims=(1,),
            start_index_map=(1,),
            operand_batching_dims=(0,),
            start_indices_batching_dims=(0,),
        ),
        slice_sizes=(1, 1),
        mode=lax.GatherScatterMode.PROMISE_IN_BOUNDS,
    )


def spread(row):
    return jnp.broadcast_to(row, (8, LANES))


def cols(tile):
    if isinstance(tile, int):
        return pl.ds(tile * LANES, LANES)
    return pl.ds(pl.multiple_of(tile * LANES, LANES), LANES)


def leavers(up_ref, down_ref):
    place = lax.broadcasted_iota(I32, (8, LANES), 1) & 15
    index = jnp.zeros((8, LANES), I32)
    for j in range(8):
        index = jnp.where(place == j, up_ref[j], index)
        index = jnp.where(place == 8 + j, down_ref[j], index)
    return index


def columns_of(drift_ref, noisem_ref, k):
    out = []
    for ref in (drift_ref, noisem_ref):
        block = ref[pl.ds(HALF + k, 8, stride=HALF), :]
        out += [jnp.broadcast_to(block[:, j:j + 1], (8, LANES)) for j in range(9)]
    return out


def ahead():
    return lax.shift_right_logical((64 - lax.axis_index("space")) * TILES, 6)


def pick(load, high, low):
    found = take(load(0), low)
    for tile in range(1, TILES):
        found = jnp.where(high == tile, take(load(tile), low), found)
    return found


def lists_body(up_ref, down_ref, nbr_ref, rows_ref, words_ref, codes_ref):
    at = lax.broadcasted_iota(I32, (8, LANES), 0) * LANES + lax.broadcasted_iota(I32, (8, LANES), 1)
    code = jnp.full((8, LANES), -1, I32)
    for j in range(8):
        code = jnp.where(at == up_ref[j], 8 + j, code)
        code = jnp.where(at == down_ref[j], j, code)
    codes_ref[...] = code
    lane = lax.broadcasted_iota(I32, (SLOTS, LANES), 1)
    bits = jnp.zeros((SLOTS, LANES), I32)
    for tile in range(TILES):
        block = nbr_ref[:, cols(tile)]
        empty = block == lane + tile * LANES
        rows_ref[tile] = jnp.where(empty, -1, block)
        mine = jnp.where(empty, 0, lax.shift_left(jnp.ones_like(block), lax.shift_right_logical(block, 7)))
        for step in (64, 32, 16, 8, 4, 2, 1):
            mine = mine | pltpu.roll(mine, step, axis=1)
        bits = jnp.where(lane == tile, mine, bits)
    word = jnp.where(bits != 0, 1 << 13, 0)
    previous = jnp.zeros_like(bits)
    for at in range(FAST):
        lowest = bits & -bits
        index = jnp.zeros_like(bits)
        for tile in range(1, 16):
            index = jnp.where(lowest == (1 << tile), tile, index)
        index = jnp.where(lowest == 0, previous, index)
        previous = index
        word = word | lax.shift_left(index, 4 * at)
        bits = bits & (bits - 1)
    words_ref[...] = word | jnp.where(bits != 0, 1 << 12, 0)


def kick_body(therm_hbm, noise_hbm, drift_hbm, noisem_hbm, q_ref, therm_ref, noise_ref, drift_ref, noisem_ref, sems, small):
    def copies(tile):
        at = cols(tile)
        return (
            pltpu.make_async_copy(therm_hbm.at[:, :, at], therm_ref.at[:, :, at], sems.at[0, tile]),
            pltpu.make_async_copy(noise_hbm.at[:, :, at], noise_ref.at[:, :, at], sems.at[1, tile]),
        )

    matrices = (
        pltpu.make_async_copy(drift_hbm, drift_ref, small.at[0]),
        pltpu.make_async_copy(noisem_hbm, noisem_ref, small.at[1]),
    )
    for copy in matrices:
        copy.start()
    for tile in range(TILES):
        for copy in copies(tile):
            copy.start()
    for copy in matrices:
        copy.wait()
    d0, n0 = drift_ref[0:HALF, :], noisem_ref[0:HALF, :]
    q_ref[0:HALF, ATOMS:ATOMS + LANES] = jnp.broadcast_to(d0[:, 0:1], (HALF, LANES))
    q_ref[HALF:48, ATOMS:ATOMS + LANES] = jnp.zeros((48 - HALF, LANES), F32)
    ncol = [[jnp.broadcast_to(n0[g * 8:g * 8 + 8, j:j + 1], (8, LANES)) for j in range(9)] for g in range(2)]
    diagonal = lax.broadcasted_iota(I32, (8, 9), 1) == lax.broadcasted_iota(I32, (8, 9), 0) + 1
    dcol = []
    for k in range(HALF):
        row = jnp.where(diagonal, jnp.broadcast_to(d0[k:k + 1, :], (8, 9)), 0.0)
        dcol.append(jnp.broadcast_to(jnp.sum(row, axis=1, keepdims=True), (8, LANES)))
    sub = lax.broadcasted_iota(I32, (8, LANES), 0)
    m4, m2, m1 = sub < 4, (sub & 2) == 0, (sub & 1) == 0

    def tile_step(tile, carry):
        at = cols(tile)
        for copy in copies(tile):
            copy.wait()
        for c in range(3):
            for g in range(2):
                v = [therm_ref[(g * 8 + k) * 3 + c, :, at] * dcol[g * 8 + k] for k in range(8)]
                for mask, step, count in ((m4, 4, 4), (m2, 2, 2), (m1, 1, 1)):
                    merged = []
                    for k in range(count):
                        a, b = v[k], v[k + count]
                        z = jnp.where(mask, b, a)
                        if step == 4:
                            moved = pltpu.roll(z, 4, axis=0)
                        else:
                            moved = jnp.where(mask, pltpu.roll(z, 8 - step, axis=0), pltpu.roll(z, step, axis=0))
                        merged.append(jnp.where(mask, a, b) + moved)
                    v = merged
                total = v[0]
                for j in range(9):
                    total = total + ncol[g][j] * noise_ref[(j * 3 + c) * 2 + g, :, at]
                q_ref[pl.ds(c * HALF + g * 8, 8), at] = total
        return carry

    lax.fori_loop(0, TILES, tile_step, 0)


def modes_body(up_ref, down_ref, pos_ref, mom_ref, ppos_ref, pmom_ref, const_ref, therm_ref, noise_ref, drift_ref,
               noisem_ref, modes_ref, part_ref, tcol, ncol):
    forward = const_ref[lax.axis_index("bead"), 0:BEADS, :]
    for c in range(3):
        r = slice(c * HALF, c * HALF + HALF)
        for at, (mine, other) in enumerate(((pos_ref, ppos_ref), (mom_ref, pmom_ref))):
            both = jnp.concatenate([mine[r, :], other[r, :]], axis=0)
            modes_ref[c, at] = jnp.dot(forward, both, precision=HIGHEST, preferred_element_type=F32)
    leave = leavers(up_ref, down_ref)
    high, low = lax.shift_right_logical(leave, 7), leave & 127

    def therm_step(g, carry):
        tcol[g] = pick(lambda t: therm_ref[g, :, cols(t)], high, low)
        return carry

    def noise_step(g, carry):
        ncol[g] = pick(lambda t: noise_ref[g, :, cols(t)], high, low)
        return carry

    lax.fori_loop(0, 48, therm_step, 0, unroll=12)
    lax.fori_loop(0, 54, noise_step, 0, unroll=18)
    for k in range(HALF):
        column = columns_of(drift_ref, noisem_ref, k)
        for c in range(3):
            total = None
            for j in range(8):
                term = column[1 + j] * spread(tcol[k * 3 + c, j:j + 1, :])
                total = term if total is None else total + term
            for j in range(9):
                total = total + column[9 + j] * spread(ncol[(j * 3 + c) * 2 + k // 8, k % 8:k % 8 + 1, :])
            part_ref[k * 3 + c] = total


def beads_body(up_ref, down_ref, modes_ref, q_ref, pq_ref, const_ref, part_ref, drift_ref, gup_ref, gdown_ref,
               pos_ref, mom_ref, mm_ref, ubuf_ref, dbuf_ref, upack_ref, dpack_ref, packs):
    core = lax.axis_index("bead")
    table = const_ref[core, 48:80, :]
    d00 = jnp.concatenate([q_ref[0:HALF, ATOMS:ATOMS + 1], pq_ref[0:HALF, ATOMS:ATOMS + 1]], axis=0)
    cosine, ratio, stiff = table[:, 0:1], table[:, 1:2], table[:, 2:3]
    backward = const_ref[core, 32:48, :]
    for c in range(3):
        r = slice(c * HALF, c * HALF + HALF)
        mode_pos, mode_mom = modes_ref[c, 0], modes_ref[c, 1]
        kicked = d00 * mode_mom + jnp.concatenate([q_ref[r, 0:ATOMS], pq_ref[r, 0:ATOMS]], axis=0)
        free_pos = cosine * mode_pos + ratio * kicked
        free_mom = cosine * kicked - stiff * mode_pos
        pos_ref[r, :] = jnp.dot(backward, free_pos, precision=HIGHEST, preferred_element_type=F32)
        mom_ref[r, :] = jnp.dot(backward, free_mom, precision=HIGHEST, preferred_element_type=F32)
        mm_ref[r, :] = mode_mom[0:HALF]

    for buf, ghost_ref in ((ubuf_ref, gup_ref), (dbuf_ref, gdown_ref)):
        for tile in range(GHOST_TILES):
            index = jnp.broadcast_to(ghost_ref[tile * LANES:tile * LANES + LANES].reshape(1, LANES), (8, LANES))
            high, low = lax.shift_right_logical(index, 7), index & 127
            for g in range(6):
                at = tile * 48 + g * 8
                buf[at:at + 8, :] = pick(lambda t: pos_ref[g * 8:g * 8 + 8, cols(t)], high, low)
            code = jnp.full((8, LANES), -1.0, F32)
            for j in range(8):
                code = jnp.where(index == up_ref[j], 8.0 + j, code)
                code = jnp.where(index == down_ref[j], 0.0 + j, code)
            buf[256 + tile:257 + tile, :] = code[0:1, :]
        buf[260:264, :] = jnp.zeros((4, LANES), F32)

    leave = leavers(up_ref, down_ref)
    high, low = lax.shift_right_logical(leave, 7), leave & 127
    group = lax.shift_right_logical(lax.broadcasted_iota(I32, (8, LANES), 1), 4)
    packed = [jnp.zeros((8, LANES), F32) for _ in range(8)]

    def put(at, value):
        packed[at // 8] = jnp.where(group == at % 8, value, packed[at // 8])

    for g in range(6):
        put(g, pick(lambda t: pos_ref[g * 8:g * 8 + 8, cols(t)], high, low))
        put(6 + g, pick(lambda t: mom_ref[g * 8:g * 8 + 8, cols(t)], high, low))
        packs[g] = pick(lambda t: mm_ref[g * 8:g * 8 + 8, cols(t)], high, low)
    for k in range(HALF):
        column = jnp.broadcast_to(drift_ref[pl.ds(HALF + k, 8, stride=HALF), 0:1], (8, LANES))
        for c in range(3):
            row = spread(packs[c * 2 + k // 8, k % 8:k % 8 + 1, :])
            put(12 + k * 3 + c, part_ref[k * 3 + c] + column * row)
    for buf in (ubuf_ref, dbuf_ref):
        for at in range(8):
            buf[192 + at * 8:200 + at * 8, :] = packed[at]
    upack_ref[...] = packed[0]
    dpack_ref[...] = packed[0]


def aux_work(first, last, therm_ref, noise_ref, mm_ref, drift_ref, noisem_ref, aux_ref):
    for k in range(HALF):
        column = columns_of(drift_ref, noisem_ref, k)

        def tile_step(tile, carry):
            at = cols(tile)
            for c in range(3):
                row = c * HALF + k
                total = column[0] * spread(mm_ref[row:row + 1, at])
                for j in range(8):
                    total = total + column[1 + j] * spread(therm_ref[k * 3 + c, j:j + 1, at])
                for j in range(9):
                    total = total + column[9 + j] * spread(noise_ref[(j * 3 + c) * 2 + k // 8, k % 8:k % 8 + 1, at])
                aux_ref[k * 3 + c, :, at] = total
            return carry

        lax.fori_loop(first, last, tile_step, 0)


def aux_first(therm_ref, noise_ref, mm_ref, drift_ref, noisem_ref, buf_in, pack_in, aux_ref, buf_out, pack_out):
    @pl.when(ahead() > 0)
    def _():
        aux_work(0, ahead(), therm_ref, noise_ref, mm_ref, drift_ref, noisem_ref, aux_ref)


def aux_second(therm_ref, noise_ref, mm_ref, drift_ref, noisem_ref, aux_ref):
    @pl.when(ahead() < TILES)
    def _():
        aux_work(ahead(), TILES, therm_ref, noise_ref, mm_ref, drift_ref, noisem_ref, aux_ref)


def force_body(words_vmem, codes, nbr_ref, pos_ref, mom_ref, aux_ref, aux2_ref, pack_ref, low_ref, high_ref,
               low2_ref, high2_ref, moved_hbm, momout_hbm, auxout_hbm, table, aux, moved_ref, momout_ref, words_ref,
               sems, tile_sems):
    fetch = pltpu.make_async_copy(words_vmem, words_ref, sems.at[0])
    fetch.start()
    lane = lax.broadcasted_iota(I32, (8, LANES), 1)
    from_low = (lane & 15) < 8
    packed = [
        jnp.where(from_low, low_ref[192 + at * 8:200 + at * 8, :], high_ref[192 + at * 8:200 + at * 8, :])
        for at in range(8)
    ]

    def own_tile(aux_from, tile, carry):
        at = cols(tile)
        mine = spread(codes[pl.ds(tile, 1), :])
        comes, base = mine >= 0, jnp.maximum(mine, 0)
        lanes = [base + 16 * m for m in range(8)]
        for g in range(6):
            r = slice(g * 8, g * 8 + 8)
            new = jnp.where(comes, take(packed[0], lanes[g]), pos_ref[r, at])
            table[tile, r, :] = new
            moved_ref[r, at] = new
            place = 6 + g
            momout_ref[r, at] = jnp.where(comes, take(packed[place // 8], lanes[place % 8]), mom_ref[r, at])
        for g in range(48):
            place = 12 + g
            aux[g, :, at] = jnp.where(comes, take(packed[place // 8], lanes[place % 8]), aux_from[g, :, at])
        return carry

    lax.fori_loop(0, ahead(), functools.partial(own_tile, aux_ref), 0)
    lax.fori_loop(ahead(), TILES, functools.partial(own_tile, aux2_ref), 0)
    outs = (
        pltpu.make_async_copy(moved_ref, moved_hbm, sems.at[1]),
        pltpu.make_async_copy(aux, auxout_hbm, sems.at[2]),
    )
    for out in outs:
        out.start()

    for side, (buf, source) in enumerate((
        (low_ref, jnp.where(from_low, low2_ref[...], pack_ref[...])),
        (high_ref, jnp.where(from_low, pack_ref[...], high2_ref[...])),
    )):
        for tile in range(GHOST_TILES):
            row = 256 + tile
            mine = spread(buf[row:row + 1, :]).astype(I32)
            comes, base = mine >= 0, jnp.maximum(mine, 0)
            for g in range(6):
                r = slice(g * 8, g * 8 + 8)
                old = buf[tile * 48 + g * 8:tile * 48 + g * 8 + 8, :]
                table[TILES + side * GHOST_TILES + tile, r, :] = jnp.where(comes, take(source, base + 16 * g), old)

    fetch.wait()

    def leave(tile):
        at = cols(tile)
        return pltpu.make_async_copy(momout_ref.at[:, at], momout_hbm.at[:, at], tile_sems.at[tile])

    def atom_tile(tile, carry):
        at = cols(tile)
        own = [table[tile, g * 8:g * 8 + 8, :] for g in range(6)]

        def pull(found, high, low, place):
            hit = high == place
            return [jnp.where(hit, take(table[place, g * 8:g * 8 + 8, :], low), found[g]) for g in range(6)]

        def push(total, found):
            done = list(total)
            for half in range(2):
                d = [own[2 * c + half] - found[2 * c + half] for c in range(3)]
                weight = jnp.exp((d[0] * d[0] + d[1] * d[1] + d[2] * d[2]) * (-0.5 / core_width))
                for c in range(3):
                    done[2 * c + half] = done[2 * c + half] + d[c] * weight
            return tuple(done)

        def chunk(number, total):
            first = number * CHUNK
            words = [words_ref[first + u, tile] for u in range(CHUNK)]
            seen = words[0]
            for word in words[1:]:
                seen = seen | word

            def index_of(u):
                index = spread(nbr_ref[tile, pl.ds(first + u, 1), :])
                return index, lax.shift_right_arithmetic(index, 7), index & 127

            def fast(total):
                for u in range(CHUNK):
                    _, high, low = index_of(u)
                    found = own
                    for at_most in range(FAST):
                        place = lax.shift_right_logical(words[u], 4 * at_most) & 15
                        found = pull(found, high, low, place)
                    total = push(total, found)
                return total

            def slow(total):
                def one(u, total):
                    _, high, low = index_of(u)
                    found = lax.fori_loop(0, 16, lambda place, found: tuple(pull(found, high, low, place)), tuple(own))
                    return push(total, found)

                return lax.fori_loop(0, CHUNK, one, total)

            def some(total):
                return lax.cond((seen & (1 << 12)) != 0, slow, fast, total)

            return lax.cond((seen & (1 << 13)) != 0, some, lambda total: total, total)

        zero = jnp.zeros((8, LANES), F32)
        total = lax.fori_loop(0, SLOTS // CHUNK, chunk, (zero,) * 6)
        for g in range(6):
            r = slice(g * 8, g * 8 + 8)
            momout_ref[r, at] = momout_ref[r, at] + kick_scale * total[g]
        leave(tile).start()
        return carry

    lax.fori_loop(0, TILES, atom_tile, 0)
    for out in outs:
        out.wait()
    for tile in range(TILES):
        leave(tile).wait()


def per_device(positions, momenta, thermostat, white_noise, drift_matrix, noise_matrix, leave_up, leave_down,
               ghost_up, ghost_down, neighbours):
    pos = positions.transpose(1, 0, 2).reshape(48, ATOMS)
    mom = momenta.transpose(1, 0, 2).reshape(48, ATOMS)
    therm = thermostat.transpose(0, 2, 1, 3).reshape(48, 8, ATOMS)
    noise = white_noise.transpose(1, 2, 0, 3).reshape(54, 8, ATOMS)
    drift = drift_matrix.transpose(1, 0, 2).reshape(144, 9)
    noisem = noise_matrix.transpose(1, 0, 2).reshape(144, 9)
    const = jnp.asarray(CONSTANTS)

    other_pos = shifted(pos, "bead", 1)
    other_mom = shifted(mom, "bead", 1)
    held = [pltpu.with_memory_space_constraint(x, pltpu.HBM) for x in (therm, noise, drift, noisem)]
    q, therm, noise, drift, noisem = call(
        kick_body,
        [struct(48, ATOMS + LANES), struct(48, 8, ATOMS), struct(54, 8, ATOMS), struct(144, 9), struct(144, 9)],
        held, specs=[HBM] * 4,
        scratch=[pltpu.SemaphoreType.DMA((2, TILES)), pltpu.SemaphoreType.DMA((2,))], flops=4000000, nbytes=3600000,
    )
    other_q = shifted(q, "bead", 1)
    modes, part = call(
        modes_body,
        [struct(3, 2, BEADS, ATOMS), struct(48, 8, LANES)],
        [leave_up, leave_down, pos, mom, other_pos, other_mom, const, therm, noise, drift, noisem],
        specs=[SMEM] * 2 + [VMEM] * 9,
        scratch=[pltpu.VMEM((48, 8, LANES), F32), pltpu.VMEM((54, 8, LANES), F32)],
        flops=8000000, nbytes=4000000,
    )
    bead_pos, bead_mom, mode_mom, up_buf, down_buf, up_pack, down_pack = call(
        beads_body,
        [struct(48, ATOMS)] * 3 + [struct(264, LANES)] * 2 + [struct(8, LANES)] * 2,
        [leave_up, leave_down, modes, q, other_q, const, part, drift, ghost_up, ghost_down],
        specs=[SMEM] * 2 + [VMEM] * 8,
        scratch=[pltpu.VMEM((6, 8, LANES), F32)],
        flops=8000000, nbytes=2000000,
    )
    low = shifted(up_buf, "space", 1)
    low2 = shifted(up_pack, "space", 2)
    work = [therm, noise, mode_mom, drift, noisem]
    aux, down_buf, down_pack = call(
        aux_first, [struct(48, 8, ATOMS), struct(264, LANES), struct(8, LANES)], work + [down_buf, down_pack],
        specs=[VMEM] * 5 + [ANY] * 2, out_specs=[VMEM, ANY, ANY], alias={5: 1, 6: 2}, flops=1000, nbytes=1000,
    )
    high = shifted(down_buf, "space", -1)
    high2 = shifted(down_pack, "space", -2)
    (aux2,) = call(aux_second, [struct(48, 8, ATOMS)], work, flops=16000000, nbytes=5000000)
    rows, words, codes = call(
        lists_body,
        [struct(TILES, SLOTS, LANES, dtype=I32), struct(SLOTS, LANES, dtype=I32), struct(8, LANES, dtype=I32)],
        [leave_up, leave_down, neighbours], specs=[SMEM, SMEM, VMEM],
        flops=1000000, nbytes=300000,
    )
    moved, slab, out_aux = call(
        force_body,
        [struct(48, ATOMS), struct(48, ATOMS), struct(48, 8, ATOMS)],
        [words, codes, rows, bead_pos, bead_mom, aux, aux2, up_pack, low, high, low2, high2],
        out_specs=[HBM] * 3,
        scratch=[
            pltpu.VMEM((2 * TILES, 48, LANES), F32),
            pltpu.VMEM((48, 8, ATOMS), F32),
            pltpu.VMEM((48, ATOMS), F32),
            pltpu.VMEM((48, ATOMS), F32),
            pltpu.SMEM((SLOTS, LANES), I32),
            pltpu.SemaphoreType.DMA((3,)),
            pltpu.SemaphoreType.DMA((TILES,)),
        ],
        flops=30000000, nbytes=4000000,
    )
    moved = moved.reshape(3, HALF, ATOMS).transpose(1, 0, 2)
    slab = slab.reshape(3, HALF, ATOMS).transpose(1, 0, 2)
    out_aux = out_aux.reshape(HALF, 3, 8, ATOMS).transpose(0, 2, 1, 3)
    return (moved, slab, out_aux)


def solution(mesh):
    in_specs = (
        P("bead", None, "space"),
        P("bead", None, "space"),
        P("bead", None, None, "space"),
        P("bead", None, None, "space"),
        P("bead", None, None),
        P("bead", None, None),
        P("space"),
        P("space"),
        P("space"),
        P("space"),
        P(None, "space"),
    )
    out_specs = (P("bead", None, "space"), P("bead", None, "space"), P("bead", None, None, "space"))

    return jax.shard_map(per_device, mesh=mesh, in_specs=in_specs, out_specs=out_specs, check_vma=False)
```

time: 674 us -> 44.3 us (0.07); the launches traced: 664 us -> 43.5 us
  local copies, waits for them, and re-layouts: 367 us -> 0.04 us
  other arithmetic: 225 us -> 0 us
  Pallas kernels: 0 us -> 25.8 us
  waiting for transfers between devices: 27 us -> 8.35 us
  between operations: 14.8 us -> 0.79 us
  matrix products: 14 us -> 0 us
  starting transfers between devices: 15.6 us -> 8.5 us
    gather x7 -> x0, local copies, waits for them, and re-layouts: 264 us -> none  [the longest x1 238 us: per_device(): gathered = slab_table[:, :, neighbours]]
    reduce_sum x2 -> x0, other arithmetic: 192 us -> none  [the longest x1 163 us: pair_forces(): weight = jnp.exp(-jnp.sum(offset * offset, axis=-3) / (2.0 * core_width))]
    pallas_call x0 -> x7, Pallas kernels: none -> 25.8 us  [call(): pl.pallas_call(body, out_shape=outs, in_specs=specs or [VMEM] * len(args)...]
    slice x4 -> x0, local copies, waits for them, and re-layouts: 23.4 us -> none  [the longest x2 14.4 us: per_device(): moved_aux = stacked[:, 6:].reshape(thermostat.shape)]
    concatenate x2 -> x0, local copies, waits for them, and re-layouts: 23.2 us -> none  [the longest x1 15.7 us: per_device(): jnp.concatenate([moved_pos, lower_ghosts, upper_ghosts], axis=2)]
    reduce_sum x2 -> x0, local copies, waits for them, and re-layouts: 19.7 us -> none  [the longest x1 11.1 us: pair_forces(): weight = jnp.exp(-jnp.sum(offset * offset, axis=-3) / (2.0 * core_width))]
    reduce_scatter x2 -> x0, waiting for transfers between devices: 19.3 us -> none  [transform(): lax.psum_scatter(jnp.einsum('ob,bcn->ocn', picked, values, precision=high...]
    concatenate x2 -> x0, other arithmetic: 16.5 us -> none  [the longest x1 14 us: per_device(): jnp.concatenate([moved_pos, lower_ghosts, upper_ghosts], axis=2)]
  transfers between devices with their start and end apart: 6 -> 7, of which waited for: 3 -> 4; matrix products, arithmetic and copies ran while one was open for 9% -> 0% of each run, Pallas kernels for 0% -> 10%
where the time goes in v1:
time: 44.3 us; the launch traced here: 43.5 us
  Pallas kernels  25.8 us (58%)
  starting transfers between devices  8.5 us (19%)
  waiting for transfers between devices  8.35 us (19%)
  between operations  0.79 us (2%)
    pallas_call x7, Pallas kernels, call(): pl.pallas_call(body, out_shape=outs, in_specs=specs or [VMEM] * len(args)...  25.8 us
    ppermute x7, starting transfers between devices, shifted(): lax.ppermute(array, axis, [(i, (i + by) % devices) for i in range(devices)])  8.5 us
    ppermute x7, waiting for transfers between devices, shifted(): lax.ppermute(array, axis, [(i, (i + by) % devices) for i in range(devices)])  8.35 us
  transfers between devices with their start and end apart: 7, of which 4 were waited for; matrix products, arithmetic and copies ran while one was open for 0% of the time, Pallas kernels for 10%

profile of v1, /device:TPU:0, one launch (start us, length us, event | category | flops | bytes accessed | tf_op | source)
XLA Modules:
  0.0 43.5 jit_solution(9777109491283147553)
XLA Ops:
  0.6 0.0 copy-start.1
  0.6 0.0 copy-start.2
  0.7 0.0 copy-start
  0.7 0.0 copy-start.4
  0.7 0.0 copy-start.5
  0.7 3.0 %shard_map.140 = (f32[48,1152]{1,0:T(8,128)S(1)}, f32[48,8,1024]{2,1,0:T(8,128)S(1)}, f32[54,8,1024]{2,1,0:T(8,128)S(1)}, f32[144,9]{1,0:T(8,128)S(1)}, f32[144,9]{1,0:T(8,128)S(1)}) custom-call(f32[48,8,1024]{2,1,0:T(8,128)} %bitcast.32, f32[54,8,1024]{2,1,0:T(8,128)} %bitcast.31, f32[144,9]{1,0:T(8,128)} %bitcast.33, f32[144,9]{1,0:T(8,128)} %bitcast.34), custom_call_target="tpu_custom_call" | custom-call | flops 4000000 | bytes 3600000 | tf_op jit(solution)/shard_map/pallas_call | solution.py:62
  3.7 0.1 collective-permute-start.2
  3.7 0.0 copy-done.1
  3.8 0.5 %collective-permute-start = (f32[48,1024]{1,0:T(8,128)S(1)}, f32[48,1024]{1,0:T(8,128)S(1)}, u32[]{:S(2)}, u32[]{:S(2)}) collective-permute-start(f32[48,1024]{1,0:T(8,128)S(1)} %bitcast.27), channel_id=1, source_target_pairs={{0,64},{64,0},{1,65},{65,1},{2,66},{66,2},{3,67},{67,3},{4,68},{68... | collective-permute-start | bytes 589832 | tf_op jit(solution)/shard_map/ppermute | solution.py:80
  4.3 0.1 collective-permute-start.1
  4.4 1.1 %collective-permute-done.ppos_ref = f32[48,1024]{1,0:T(8,128)S(1)} collective-permute-done((f32[48,1024]{1,0:T(8,128)S(1)}, f32[48,1024]{1,0:T(8,128)S(1)}, u32[]{:S(2)}, u32[]{:S(2)}) %collective-permute-start) | collective-permute-done | bytes 196640 | tf_op jit(solution)/shard_map/ppermute | solution.py:80
  5.5 0.3 collective-permute-done.1.pmom_ref
  5.8 0.0 copy-done
  5.8 0.0 copy-start.6
  5.8 0.0 copy-start.7
  5.8 3.2 %shard_map.141 = (f32[3,2,32,1024]{3,2,1,0:T(8,128)S(1)}, f32[48,8,128]{2,1,0:T(8,128)S(1)}) custom-call(s32[8]{0:T(128)S(1)} %copy-done.4, s32[8]{0:T(128)S(1)} %copy-done.5, f32[48,1024]{1,0:T(8,128)S(1)} %bitcast.28, f32[48,1024]{1,0:T(8,128)S(1)} %bitcast.30, f32[48,1024]{1,0:T(8,128)S(1)} %collective-permute-done.ppos_ref, ...), custom_call_target="tpu_custom_call" | custom-call | flops 8000000 | bytes 4000000 | tf_op jit(solution)/shard_map/pallas_call | solution.py:62
  9.0 0.0 collective-permute-done.2.pq_ref
  9.0 0.0 copy-done.6
  9.0 0.0 copy-done.7
  9.0 1.9 %shard_map.142 = (f32[48,1024]{1,0:T(8,128)S(1)}, f32[48,1024]{1,0:T(8,128)S(1)}, f32[48,1024]{1,0:T(8,128)S(1)}, f32[264,128]{1,0:T(8,128)S(1)}, f32[264,128]{1...) custom-call(s32[8]{0:T(128)S(1)} %copy-done.4, s32[8]{0:T(128)S(1)} %copy-done.5, ...), custom_call_target="tpu_custom_call" | custom-call | flops 8000000 | bytes 2000000 | tf_op jit(solution)/shard_map/pallas_call | solution.py:62
  10.9 0.0 copy-start.3
  10.9 4.6 %shard_map.143 = (f32[48,8,1024]{2,1,0:T(8,128)S(1)}, f32[264,128]{1,0:T(8,128)S(1)}, f32[8,128]{1,0:T(8,128)S(1)}) custom-call(f32[48,8,1024]{2,1,0:T(8,128)S(1)} %get-tuple-element.29.therm_ref, f32[54,8,1024]{2,1,0:T(8,128)S(1)} %get-tuple-element.30.noise_ref, ...), custom_call_target="tpu_custom_call", output_to_operand_aliasing={{1}: (5, {}), {2}: (6, {})} | custom-call | flops 1000 | bytes 1000 | tf_op jit(solution)/shard_map/pallas_call | solution.py:62
  15.5 4.3 %collective-permute-start.4 = (f32[264,128]{1,0:T(8,128)S(1)}, f32[264,128]{1,0:T(8,128)S(1)}, u32[]{:S(2)}, u32[]{:S(2)}) collective-permute-start(f32[264,128]{1,0:T(8,128)S(1)} %get-tuple-element.44), channel_id=1, source_target_pairs={{0,63},{1,0},{2,1},{3,2},{4,3},{5,4},{6,5},{7,6},{8,7},{9,8},{10,9... | collective-permute-start | bytes 405512 | tf_op jit(solution)/shard_map/ppermute | solution.py:80
  19.8 0.0 collective-permute-start.3
  19.8 2.3 %collective-permute-start.6 = (f32[8,128]{1,0:T(8,128)S(1)}, f32[8,128]{1,0:T(8,128)S(1)}, u32[]{:S(2)}, u32[]{:S(2)}) collective-permute-start(f32[8,128]{1,0:T(8,128)S(1)} %get-tuple-element.45), channel_id=1, source_target_pairs={{0,62},{1,63},{2,0},{3,1},{4,2},{5,3},{6,4},{7,5},{8,6},{9,7},{10,... | collective-permute-start | bytes 12296 | tf_op jit(solution)/shard_map/ppermute | solution.py:80
  22.1 1.3 %collective-permute-start.5 = (f32[8,128]{1,0:T(8,128)S(1)}, f32[8,128]{1,0:T(8,128)S(1)}, u32[]{:S(2)}, u32[]{:S(2)}) collective-permute-start(f32[8,128]{1,0:T(8,128)S(1)} %get-tuple-element.42.pack_ref), channel_id=1, source_target_pairs={{0,2},{1,3},{2,4},{3,5},{4,6},{5,7},{6,8},{7,9},{8,10},{9,11},{10,... | collective-permute-start | bytes 12296 | tf_op jit(solution)/shard_map/ppermute | solution.py:80
  23.3 1.1 %shard_map.139 = (s32[8,32,128]{2,1,0:T(8,128)S(1)}, s32[32,128]{1,0:T(8,128)S(1)}, s32[8,128]{1,0:T(8,128)S(1)}) custom-call(s32[8]{0:T(128)S(1)} %copy-done.4, s32[8]{0:T(128)S(1)} %copy-done.5, s32[32,1024]{1,0:T(8,128)S(1)} %copy-done.3), custom_call_target="tpu_custom_call" | custom-call | flops 1000000 | bytes 300000 | tf_op jit(solution)/shard_map/pallas_call | solution.py:62
  24.5 0.4 collective-permute-done.6.high2_ref
  24.9 6.5 %collective-permute-done.5.low2_ref = f32[8,128]{1,0:T(8,128)S(1)} collective-permute-done((f32[8,128]{1,0:T(8,128)S(1)}, f32[8,128]{1,0:T(8,128)S(1)}, u32[]{:S(2)}, u32[]{:S(2)}) %collective-permute-start.5) | collective-permute-done | bytes 4128 | tf_op jit(solution)/shard_map/ppermute | solution.py:80
  31.4 0.0 collective-permute-done.4.high_ref
  31.4 0.0 collective-permute-done.3.low_ref
  31.4 12.0 %shard_map.145 = (f32[48,1024]{1,0:T(8,128)}, f32[48,1024]{1,0:T(8,128)}, f32[48,8,1024]{2,1,0:T(8,128)}) custom-call(s32[32,128]{1,0:T(8,128)S(1)} %get-tuple-element.26.words_vmem, s32[8,128]{1,0:T(8,128)S(1)} %get-tuple-element.27.codes, s32[8,32,128]{2,1,0:T(8,128)S(1)} %get-tuple-element.28.nbr_ref, f32[48,1024]{1,0:T(8,128)S(1)} %get-tuple-element.36.pos_ref, ...), custom_call_target="tpu_custom_call" | custom-call | flops 30000000 | bytes 4000000 | tf_op jit(solution)/shard_map/pallas_call | solution.py:62
  (5 shorter events, 0.0 us)
Async XLA Ops:
  0.6 3.1 %copy-start.1 = (f32[16,3,1024]{2,0,1:T(8,128)S(1)}, f32[16,3,1024]{2,0,1:T(8,128)}, u32[]{:S(2)}) copy-start(f32[16,3,1024]{2,0,1:T(8,128)} %param.12) | copy-start | bytes 589828
  0.6 3.6 %copy-start.2 = (f32[16,3,1024]{2,0,1:T(8,128)S(1)}, f32[16,3,1024]{2,0,1:T(8,128)}, u32[]{:S(2)}) copy-start(f32[16,3,1024]{2,0,1:T(8,128)} %param.13) | copy-start | bytes 589828
  0.7 5.1 %copy-start = (f32[2,80,32]{2,1,0:T(8,128)S(1)}, f32[2,80,32]{2,1,0:T(8,128)}, u32[]{:S(2)}) copy-start(f32[2,80,32]{2,1,0:T(8,128)} %constant.2.clone.const_ref) | copy-start | bytes 61444
  0.7 5.1 %copy-start.4 = (s32[8]{0:T(128)S(1)}, s32[8]{0:T(128)}, u32[]{:S(2)}) copy-start(s32[8]{0:T(128)} %up_ref.5) | copy-start | bytes 100
  0.7 5.1 %copy-start.5 = (s32[8]{0:T(128)S(1)}, s32[8]{0:T(128)}, u32[]{:S(2)}) copy-start(s32[8]{0:T(128)} %down_ref.5) | copy-start | bytes 100
  3.7 5.4 %collective-permute-start.2 = (f32[48,1152]{1,0:T(8,128)S(1)}, f32[48,1152]{1,0:T(8,128)S(1)}, u32[]{:S(2)}, u32[]{:S(2)}) collective-permute-start(f32[48,1152]{1,0:T(8,128)S(1)} %get-tuple-element.34.q_ref), channel_id=1, source_target_pairs={{0,64},{64,0},{1,65},{65,1},{2,66},{66,2},{3,67},{67,3},{4,68},{68... | collective-permute-start | bytes 663560 | tf_op jit(solution)/shard_map/ppermute | solution.py:80
  3.8 1.7 %collective-permute-start = (f32[48,1024]{1,0:T(8,128)S(1)}, f32[48,1024]{1,0:T(8,128)S(1)}, u32[]{:S(2)}, u32[]{:S(2)}) collective-permute-start(f32[48,1024]{1,0:T(8,128)S(1)} %bitcast.27), channel_id=1, source_target_pairs={{0,64},{64,0},{1,65},{65,1},{2,66},{66,2},{3,67},{67,3},{4,68},{68... | collective-permute-start | bytes 589832 | tf_op jit(solution)/shard_map/ppermute | solution.py:80
  4.3 1.5 %collective-permute-start.1 = (f32[48,1024]{1,0:T(8,128)S(1)}, f32[48,1024]{1,0:T(8,128)S(1)}, u32[]{:S(2)}, u32[]{:S(2)}) collective-permute-start(f32[48,1024]{1,0:T(8,128)S(1)} %bitcast.29), channel_id=1, source_target_pairs={{0,64},{64,0},{1,65},{65,1},{2,66},{66,2},{3,67},{67,3},{4,68},{68... | collective-permute-start | bytes 589832 | tf_op jit(solution)/shard_map/ppermute | solution.py:80
  5.8 3.2 %copy-start.6 = (s32[512]{0:T(512)S(1)}, s32[512]{0:T(512)}, u32[]{:S(2)}) copy-start(s32[512]{0:T(512)} %gup_ref.1) | copy-start | bytes 6148
  5.8 3.2 %copy-start.7 = (s32[512]{0:T(512)S(1)}, s32[512]{0:T(512)}, u32[]{:S(2)}) copy-start(s32[512]{0:T(512)} %gdown_ref.1) | copy-start | bytes 6148
  10.9 12.4 %copy-start.3 = (s32[32,1024]{1,0:T(8,128)S(1)}, s32[32,1024]{1,0:T(8,128)}, u32[]{:S(2)}) copy-start(s32[32,1024]{1,0:T(8,128)} %nbr_ref.1) | copy-start | bytes 393220
  15.5 15.9 %collective-permute-start.4 = (f32[264,128]{1,0:T(8,128)S(1)}, f32[264,128]{1,0:T(8,128)S(1)}, u32[]{:S(2)}, u32[]{:S(2)}) collective-permute-start(f32[264,128]{1,0:T(8,128)S(1)} %get-tuple-element.44), channel_id=1, source_target_pairs={{0,63},{1,0},{2,1},{3,2},{4,3},{5,4},{6,5},{7,6},{8,7},{9,8},{10,9... | collective-permute-start | bytes 405512 | tf_op jit(solution)/shard_map/ppermute | solution.py:80
  19.8 11.6 %collective-permute-start.3 = (f32[264,128]{1,0:T(8,128)S(1)}, f32[264,128]{1,0:T(8,128)S(1)}, u32[]{:S(2)}, u32[]{:S(2)}) collective-permute-start(f32[264,128]{1,0:T(8,128)S(1)} %get-tuple-element.43), channel_id=1, source_target_pairs={{0,1},{1,2},{2,3},{3,4},{4,5},{5,6},{6,7},{7,8},{8,9},{9,10},{10,1... | collective-permute-start | bytes 405512 | tf_op jit(solution)/shard_map/ppermute | solution.py:80
  19.8 5.1 %collective-permute-start.6 = (f32[8,128]{1,0:T(8,128)S(1)}, f32[8,128]{1,0:T(8,128)S(1)}, u32[]{:S(2)}, u32[]{:S(2)}) collective-permute-start(f32[8,128]{1,0:T(8,128)S(1)} %get-tuple-element.45), channel_id=1, source_target_pairs={{0,62},{1,63},{2,0},{3,1},{4,2},{5,3},{6,4},{7,5},{8,6},{9,7},{10,... | collective-permute-start | bytes 12296 | tf_op jit(solution)/shard_map/ppermute | solution.py:80
  22.1 9.3 %collective-permute-start.5 = (f32[8,128]{1,0:T(8,128)S(1)}, f32[8,128]{1,0:T(8,128)S(1)}, u32[]{:S(2)}, u32[]{:S(2)}) collective-permute-start(f32[8,128]{1,0:T(8,128)S(1)} %get-tuple-element.42.pack_ref), channel_id=1, source_target_pairs={{0,2},{1,3},{2,4},{3,5},{4,6},{5,7},{6,8},{7,9},{8,10},{9,11},{10,... | collective-permute-start | bytes 12296 | tf_op jit(solution)/shard_map/ppermute | solution.py:80

commit v2 on v1

--- a/solution.py
+++ b/solution.py
@@ -1,4 +1,3 @@
-import functools
 import math
 
 import jax
@@ -17,8 +16,9 @@
 SLOTS = 32
 GHOST_TILES = 4
 LANES = 128
-FAST = 3
-CHUNK = 8
+WINDOWS = 32
+EMPTY = 4095
+CHUNK = 32
 
 cycle_rate = 0.8
 kick_scale = 0.2
@@ -30,7 +30,6 @@
 SMEM = pl.BlockSpec(memory_space=pltpu.SMEM)
 ANY = pl.BlockSpec(memory_space=pl.ANY)
 HBM = pl.BlockSpec(memory_space=pltpu.HBM)
-HIGHEST = lax.Precision.HIGHEST
 
 
 def constants():
@@ -44,18 +43,22 @@
     w = 2.0 * cycle_rate * np.sin(math.pi * np.arange(BEADS) / BEADS)
     ratio = np.where(w > 0, np.sin(w) / np.where(w > 0, w, 1.0), 1.0)
     columns = np.stack([np.cos(w), ratio, w * np.sin(w)], axis=1)
-    forward, backward, tables = [], [], []
+
+    def stacked(matrix):
+        high = matrix.astype(jnp.bfloat16)
+        low = (matrix - high.astype(np.float64)).astype(jnp.bfloat16)
+        return np.concatenate([high, high, low], axis=1)
+
+    matrices, tables = [], []
     for core in range(2):
         order = np.roll(np.arange(BEADS), -HALF * core)
-        forward.append(basis[order][:, order])
-        backward.append(basis[order][:, order[:HALF]].T)
+        forward = basis[order][:, order]
+        matrices.append(stacked(np.concatenate([forward, forward.T[:HALF]], axis=0)))
         tables.append(np.pad(columns[order], ((0, 0), (0, 5))))
-    tables = [np.pad(x, ((0, 0), (0, BEADS - 8))) for x in tables]
-    parts = [np.concatenate(x, axis=0) for x in zip(forward, backward, tables)]
-    return np.stack(parts).astype(np.float32)
-
-
-CONSTANTS = constants()
+    return np.stack(matrices), np.stack(tables).astype(np.float32)
+
+
+MATRICES, TABLES = constants()
 
 
 def call(body, outs, args, specs=None, out_specs=None, scratch=(), flops=0, nbytes=0, limit=24, alias=None):
@@ -96,6 +99,12 @@
     )
 
 
+def transform(matrix, values):
+    high = values.astype(jnp.bfloat16)
+    low = (values - high.astype(F32)).astype(jnp.bfloat16)
+    return jnp.dot(matrix, jnp.concatenate([high, low, high], axis=0), preferred_element_type=F32)
+
+
 def spread(row):
     return jnp.broadcast_to(row, (8, LANES))
 
@@ -115,16 +124,10 @@
     return index
 
 
-def columns_of(drift_ref, noisem_ref, k):
-    out = []
-    for ref in (drift_ref, noisem_ref):
-        block = ref[pl.ds(HALF + k, 8, stride=HALF), :]
-        out += [jnp.broadcast_to(block[:, j:j + 1], (8, LANES)) for j in range(9)]
-    return out
-
-
 def ahead():
-    return lax.shift_right_logical((64 - lax.axis_index("space")) * TILES, 6)
+    slab = lax.axis_index("space")
+    way = 3 * (slab & 3) + 3 * (lax.shift_right_logical(slab, 2) & 3) + 5 * lax.shift_right_logical(slab, 4)
+    return TILES - lax.shift_right_logical(way * TILES + HALF, 5)
 
 
 def pick(load, high, low):
@@ -134,38 +137,42 @@
     return found
 
 
-def lists_body(up_ref, down_ref, nbr_ref, rows_ref, words_ref, codes_ref):
-    at = lax.broadcasted_iota(I32, (8, LANES), 0) * LANES + lax.broadcasted_iota(I32, (8, LANES), 1)
-    code = jnp.full((8, LANES), -1, I32)
-    for j in range(8):
-        code = jnp.where(at == up_ref[j], 8 + j, code)
-        code = jnp.where(at == down_ref[j], j, code)
-    codes_ref[...] = code
+def make_lists(nbr_ref, rows_ref, words_ref):
     lane = lax.broadcasted_iota(I32, (SLOTS, LANES), 1)
-    bits = jnp.zeros((SLOTS, LANES), I32)
+    masks = []
     for tile in range(TILES):
         block = nbr_ref[:, cols(tile)]
-        empty = block == lane + tile * LANES
-        rows_ref[tile] = jnp.where(empty, -1, block)
-        mine = jnp.where(empty, 0, lax.shift_left(jnp.ones_like(block), lax.shift_right_logical(block, 7)))
-        for step in (64, 32, 16, 8, 4, 2, 1):
-            mine = mine | pltpu.roll(mine, step, axis=1)
-        bits = jnp.where(lane == tile, mine, bits)
-    word = jnp.where(bits != 0, 1 << 13, 0)
-    previous = jnp.zeros_like(bits)
-    for at in range(FAST):
-        lowest = bits & -bits
-        index = jnp.zeros_like(bits)
-        for tile in range(1, 16):
-            index = jnp.where(lowest == (1 << tile), tile, index)
-        index = jnp.where(lowest == 0, previous, index)
-        previous = index
-        word = word | lax.shift_left(index, 4 * at)
-        bits = bits & (bits - 1)
-    words_ref[...] = word | jnp.where(bits != 0, 1 << 12, 0)
-
-
-def kick_body(therm_hbm, noise_hbm, drift_hbm, noisem_hbm, q_ref, therm_ref, noise_ref, drift_ref, noisem_ref, sems, small):
+        mine = lax.shift_left(jnp.ones_like(block), lax.shift_right_logical(block, 6))
+        masks.append(jnp.where(block == lane + tile * LANES, 0, mine))
+    for step, count in ((64, 4), (32, 2), (16, 1)):
+        lower = (lane & step) == 0
+        merged = []
+        for at in range(count):
+            first, second = masks[at], masks[at + count]
+            other = jnp.where(lower, second, first)
+            moved = jnp.where(lower, pltpu.roll(other, LANES - step, axis=1), pltpu.roll(other, step, axis=1))
+            merged.append(jnp.where(lower, first, second) | moved)
+        masks = merged
+    bits = masks[0]
+    for step in (8, 4, 2, 1):
+        bits = bits | pltpu.roll(bits, LANES - step, axis=1)
+    window = jnp.zeros_like(bits)
+    wide = jnp.ones_like(bits)
+    for at in range(WINDOWS):
+        covered = sum(1 << ((at + i) % WINDOWS) for i in range(4))
+        covered = covered - (1 << 32) if covered >= 1 << 31 else covered
+        fits = (bits & ~covered) == 0
+        window = jnp.where(fits, at, window)
+        wide = jnp.where(fits, 0, wide)
+    words_ref[...] = window | (wide << 8) | jnp.where(bits != 0, 1 << 9, 0)
+    for tile in range(TILES):
+        block = nbr_ref[:, cols(tile)]
+        start = jnp.broadcast_to(window[:, 16 * tile:16 * tile + 1], (SLOTS, LANES)) << 6
+        rows_ref[tile] = jnp.where(block == lane + tile * LANES, EMPTY, (block - start) & 2047)
+
+
+def kick_body(therm_hbm, noise_hbm, drift_hbm, noisem_hbm, nbr_hbm, q_ref, therm_ref, noise_ref, coef_ref, rows_ref,
+              words_ref, drift_ref, noisem_ref, nbr_ref, sems, small):
     def copies(tile):
         at = cols(tile)
         return (
@@ -176,14 +183,25 @@
     matrices = (
         pltpu.make_async_copy(drift_hbm, drift_ref, small.at[0]),
         pltpu.make_async_copy(noisem_hbm, noisem_ref, small.at[1]),
+        pltpu.make_async_copy(nbr_hbm, nbr_ref, small.at[2]),
     )
     for copy in matrices:
         copy.start()
-    for tile in range(TILES):
+
+    def begin(tile, carry):
         for copy in copies(tile):
             copy.start()
+        return carry
+
+    lax.fori_loop(0, TILES, begin, 0)
     for copy in matrices:
         copy.wait()
+    make_lists(nbr_ref, rows_ref, words_ref)
+    for k in range(HALF):
+        for at, ref in enumerate((drift_ref, noisem_ref)):
+            block = ref[pl.ds(HALF + k, 8, stride=HALF), :]
+            for j in range(9):
+                coef_ref[k * 18 + at * 9 + j] = jnp.broadcast_to(block[:, j:j + 1], (8, LANES))
     d0, n0 = drift_ref[0:HALF, :], noisem_ref[0:HALF, :]
     q_ref[0:HALF, ATOMS:ATOMS + LANES] = jnp.broadcast_to(d0[:, 0:1], (HALF, LANES))
     q_ref[HALF:48, ATOMS:ATOMS + LANES] = jnp.zeros((48 - HALF, LANES), F32)
@@ -223,14 +241,13 @@
     lax.fori_loop(0, TILES, tile_step, 0)
 
 
-def modes_body(up_ref, down_ref, pos_ref, mom_ref, ppos_ref, pmom_ref, const_ref, therm_ref, noise_ref, drift_ref,
-               noisem_ref, modes_ref, part_ref, tcol, ncol):
+def modes_body(up_ref, down_ref, pos_ref, mom_ref, ppos_ref, pmom_ref, const_ref, therm_ref, noise_ref, coef_ref,
+               modes_ref, part_ref, tcol, ncol):
     forward = const_ref[lax.axis_index("bead"), 0:BEADS, :]
     for c in range(3):
         r = slice(c * HALF, c * HALF + HALF)
         for at, (mine, other) in enumerate(((pos_ref, ppos_ref), (mom_ref, pmom_ref))):
-            both = jnp.concatenate([mine[r, :], other[r, :]], axis=0)
-            modes_ref[c, at] = jnp.dot(forward, both, precision=HIGHEST, preferred_element_type=F32)
+            modes_ref[c, at] = transform(forward, jnp.concatenate([mine[r, :], other[r, :]], axis=0))
     leave = leavers(up_ref, down_ref)
     high, low = lax.shift_right_logical(leave, 7), leave & 127
 
@@ -245,21 +262,21 @@
     lax.fori_loop(0, 48, therm_step, 0, unroll=12)
     lax.fori_loop(0, 54, noise_step, 0, unroll=18)
     for k in range(HALF):
-        column = columns_of(drift_ref, noisem_ref, k)
         for c in range(3):
             total = None
             for j in range(8):
-                term = column[1 + j] * spread(tcol[k * 3 + c, j:j + 1, :])
+                term = coef_ref[k * 18 + 1 + j] * spread(tcol[k * 3 + c, j:j + 1, :])
                 total = term if total is None else total + term
             for j in range(9):
-                total = total + column[9 + j] * spread(ncol[(j * 3 + c) * 2 + k // 8, k % 8:k % 8 + 1, :])
+                row = spread(ncol[(j * 3 + c) * 2 + k // 8, k % 8:k % 8 + 1, :])
+                total = total + coef_ref[k * 18 + 9 + j] * row
             part_ref[k * 3 + c] = total
 
 
-def beads_body(up_ref, down_ref, modes_ref, q_ref, pq_ref, const_ref, part_ref, drift_ref, gup_ref, gdown_ref,
-               pos_ref, mom_ref, mm_ref, ubuf_ref, dbuf_ref, upack_ref, dpack_ref, packs):
+def beads_body(up_ref, down_ref, modes_ref, q_ref, pq_ref, const_ref, table_ref, part_ref, coef_ref, gup_ref, gdown_ref,
+               pos_ref, mom_ref, mm_ref, ubuf_ref, dbuf_ref, upack_ref, dpack_ref, codes_ref, packs):
     core = lax.axis_index("bead")
-    table = const_ref[core, 48:80, :]
+    table = table_ref[core]
     d00 = jnp.concatenate([q_ref[0:HALF, ATOMS:ATOMS + 1], pq_ref[0:HALF, ATOMS:ATOMS + 1]], axis=0)
     cosine, ratio, stiff = table[:, 0:1], table[:, 1:2], table[:, 2:3]
     backward = const_ref[core, 32:48, :]
@@ -269,8 +286,8 @@
         kicked = d00 * mode_mom + jnp.concatenate([q_ref[r, 0:ATOMS], pq_ref[r, 0:ATOMS]], axis=0)
         free_pos = cosine * mode_pos + ratio * kicked
         free_mom = cosine * kicked - stiff * mode_pos
-        pos_ref[r, :] = jnp.dot(backward, free_pos, precision=HIGHEST, preferred_element_type=F32)
-        mom_ref[r, :] = jnp.dot(backward, free_mom, precision=HIGHEST, preferred_element_type=F32)
+        pos_ref[r, :] = transform(backward, free_pos)
+        mom_ref[r, :] = transform(backward, free_mom)
         mm_ref[r, :] = mode_mom[0:HALF]
 
     for buf, ghost_ref in ((ubuf_ref, gup_ref), (dbuf_ref, gdown_ref)):
@@ -300,7 +317,7 @@
         put(6 + g, pick(lambda t: mom_ref[g * 8:g * 8 + 8, cols(t)], high, low))
         packs[g] = pick(lambda t: mm_ref[g * 8:g * 8 + 8, cols(t)], high, low)
     for k in range(HALF):
-        column = jnp.broadcast_to(drift_ref[pl.ds(HALF + k, 8, stride=HALF), 0:1], (8, LANES))
+        column = coef_ref[k * 18]
         for c in range(3):
             row = spread(packs[c * 2 + k // 8, k % 8:k % 8 + 1, :])
             put(12 + k * 3 + c, part_ref[k * 3 + c] + column * row)
@@ -309,14 +326,19 @@
             buf[192 + at * 8:200 + at * 8, :] = packed[at]
     upack_ref[...] = packed[0]
     dpack_ref[...] = packed[0]
-
-
-def aux_work(first, last, therm_ref, noise_ref, mm_ref, drift_ref, noisem_ref, aux_ref):
-    for k in range(HALF):
-        column = columns_of(drift_ref, noisem_ref, k)
-
-        def tile_step(tile, carry):
-            at = cols(tile)
+    at = lax.broadcasted_iota(I32, (8, LANES), 0) * LANES + lax.broadcasted_iota(I32, (8, LANES), 1)
+    code = jnp.full((8, LANES), -1, I32)
+    for j in range(8):
+        code = jnp.where(at == up_ref[j], 8 + j, code)
+        code = jnp.where(at == down_ref[j], j, code)
+    codes_ref[...] = code
+
+
+def aux_work(first, last, therm_ref, noise_ref, mm_ref, coef_ref, aux_ref):
+    def tile_step(tile, carry):
+        at = cols(tile)
+        for k in range(HALF):
+            column = [coef_ref[k * 18 + j] for j in range(18)]
             for c in range(3):
                 row = c * HALF + k
                 total = column[0] * spread(mm_ref[row:row + 1, at])
@@ -325,24 +347,20 @@
                 for j in range(9):
                     total = total + column[9 + j] * spread(noise_ref[(j * 3 + c) * 2 + k // 8, k % 8:k % 8 + 1, at])
                 aux_ref[k * 3 + c, :, at] = total
-            return carry
-
-        lax.fori_loop(first, last, tile_step, 0)
-
-
-def aux_first(therm_ref, noise_ref, mm_ref, drift_ref, noisem_ref, buf_in, pack_in, aux_ref, buf_out, pack_out):
-    @pl.when(ahead() > 0)
-    def _():
-        aux_work(0, ahead(), therm_ref, noise_ref, mm_ref, drift_ref, noisem_ref, aux_ref)
-
-
-def aux_second(therm_ref, noise_ref, mm_ref, drift_ref, noisem_ref, aux_ref):
-    @pl.when(ahead() < TILES)
-    def _():
-        aux_work(ahead(), TILES, therm_ref, noise_ref, mm_ref, drift_ref, noisem_ref, aux_ref)
-
-
-def force_body(words_vmem, codes, nbr_ref, pos_ref, mom_ref, aux_ref, aux2_ref, pack_ref, low_ref, high_ref,
+        return carry
+
+    lax.fori_loop(first, last, tile_step, 0)
+
+
+def aux_first(therm_ref, noise_ref, mm_ref, coef_ref, buf_in, pack_in, aux_ref, buf_out, pack_out):
+    aux_work(0, ahead(), therm_ref, noise_ref, mm_ref, coef_ref, aux_ref)
+
+
+def aux_second(done_ref, therm_ref, noise_ref, mm_ref, coef_ref, aux_ref):
+    aux_work(ahead(), TILES, therm_ref, noise_ref, mm_ref, coef_ref, aux_ref)
+
+
+def force_body(words_vmem, codes, nbr_ref, pos_ref, mom_ref, aux_ref, pack_ref, low_ref, high_ref,
                low2_ref, high2_ref, moved_hbm, momout_hbm, auxout_hbm, table, aux, moved_ref, momout_ref, words_ref,
                sems, tile_sems):
     fetch = pltpu.make_async_copy(words_vmem, words_ref, sems.at[0])
@@ -354,7 +372,7 @@
         for at in range(8)
     ]
 
-    def own_tile(aux_from, tile, carry):
+    def own_tile(tile, carry):
         at = cols(tile)
         mine = spread(codes[pl.ds(tile, 1), :])
         comes, base = mine >= 0, jnp.maximum(mine, 0)
@@ -362,17 +380,16 @@
         for g in range(6):
             r = slice(g * 8, g * 8 + 8)
             new = jnp.where(comes, take(packed[0], lanes[g]), pos_ref[r, at])
-            table[tile, r, :] = new
+            table[2 * tile, r, :] = new
             moved_ref[r, at] = new
             place = 6 + g
             momout_ref[r, at] = jnp.where(comes, take(packed[place // 8], lanes[place % 8]), mom_ref[r, at])
         for g in range(48):
             place = 12 + g
-            aux[g, :, at] = jnp.where(comes, take(packed[place // 8], lanes[place % 8]), aux_from[g, :, at])
-        return carry
-
-    lax.fori_loop(0, ahead(), functools.partial(own_tile, aux_ref), 0)
-    lax.fori_loop(ahead(), TILES, functools.partial(own_tile, aux2_ref), 0)
+            aux[g, :, at] = jnp.where(comes, take(packed[place // 8], lanes[place % 8]), aux_ref[g, :, at])
+        return carry
+
+    lax.fori_loop(0, TILES, own_tile, 0, unroll=2)
     outs = (
         pltpu.make_async_copy(moved_ref, moved_hbm, sems.at[1]),
         pltpu.make_async_copy(aux, auxout_hbm, sems.at[2]),
@@ -391,8 +408,13 @@
             for g in range(6):
                 r = slice(g * 8, g * 8 + 8)
                 old = buf[tile * 48 + g * 8:tile * 48 + g * 8 + 8, :]
-                table[TILES + side * GHOST_TILES + tile, r, :] = jnp.where(comes, take(source, base + 16 * g), old)
-
+                table[2 * (TILES + side * GHOST_TILES + tile), r, :] = jnp.where(comes, take(source, base + 16 * g), old)
+
+    for g in range(6):
+        r = slice(g * 8, g * 8 + 8)
+        rolled = [pltpu.roll(table[2 * tile, r, :], 64, axis=1) for tile in range(2 * TILES)]
+        for tile in range(2 * TILES):
+            table[2 * tile + 1, r, :] = jnp.where(lane < 64, rolled[tile], rolled[(tile + 1) % (2 * TILES)])
     fetch.wait()
 
     def leave(tile):
@@ -401,10 +423,9 @@
 
     def atom_tile(tile, carry):
         at = cols(tile)
-        own = [table[tile, g * 8:g * 8 + 8, :] for g in range(6)]
-
-        def pull(found, high, low, place):
-            hit = high == place
+        own = [table[2 * tile, g * 8:g * 8 + 8, :] for g in range(6)]
+
+        def pull(found, hit, low, place):
             return [jnp.where(hit, take(table[place, g * 8:g * 8 + 8, :], low), found[g]) for g in range(6)]
 
         def push(total, found):
@@ -418,37 +439,36 @@
 
         def chunk(number, total):
             first = number * CHUNK
-            words = [words_ref[first + u, tile] for u in range(CHUNK)]
+            words = [words_ref[first + u, 16 * tile] for u in range(CHUNK)]
             seen = words[0]
             for word in words[1:]:
                 seen = seen | word
 
-            def index_of(u):
-                index = spread(nbr_ref[tile, pl.ds(first + u, 1), :])
-                return index, lax.shift_right_arithmetic(index, 7), index & 127
-
             def fast(total):
                 for u in range(CHUNK):
-                    _, high, low = index_of(u)
-                    found = own
-                    for at_most in range(FAST):
-                        place = lax.shift_right_logical(words[u], 4 * at_most) & 15
-                        found = pull(found, high, low, place)
-                    total = push(total, found)
+                    index = spread(nbr_ref[tile, pl.ds(first + u, 1), :])
+                    high, low = lax.shift_right_logical(index, 7), index & 127
+                    place = words[u] & 31
+                    found = pull(own, high == 0, low, place)
+                    total = push(total, pull(found, high == 1, low, (place + 2) & 31))
                 return total
 
             def slow(total):
                 def one(u, total):
-                    _, high, low = index_of(u)
-                    found = lax.fori_loop(0, 16, lambda place, found: tuple(pull(found, high, low, place)), tuple(own))
+                    index = spread(nbr_ref[tile, pl.ds(first + u, 1), :])
+                    index = jnp.where(index == EMPTY, EMPTY, (index + (words_ref[first + u, 16 * tile] & 31) * 64) & 2047)
+                    high, low = lax.shift_right_logical(index, 7), index & 127
+                    found = lax.fori_loop(
+                        0, 16, lambda place, found: tuple(pull(found, high == place, low, 2 * place)), tuple(own)
+                    )
                     return push(total, found)
 
                 return lax.fori_loop(0, CHUNK, one, total)
 
             def some(total):
-                return lax.cond((seen & (1 << 12)) != 0, slow, fast, total)
-
-            return lax.cond((seen & (1 << 13)) != 0, some, lambda total: total, total)
+                return lax.cond((seen & (1 << 8)) != 0, slow, fast, total)
+
+            return lax.cond((seen & (1 << 9)) != 0, some, lambda total: total, total)
 
         zero = jnp.zeros((8, LANES), F32)
         total = lax.fori_loop(0, SLOTS // CHUNK, chunk, (zero,) * 6)
@@ -473,57 +493,58 @@
     noise = white_noise.transpose(1, 2, 0, 3).reshape(54, 8, ATOMS)
     drift = drift_matrix.transpose(1, 0, 2).reshape(144, 9)
     noisem = noise_matrix.transpose(1, 0, 2).reshape(144, 9)
-    const = jnp.asarray(CONSTANTS)
+    matrices, tables = jnp.asarray(MATRICES), jnp.asarray(TABLES)
 
     other_pos = shifted(pos, "bead", 1)
     other_mom = shifted(mom, "bead", 1)
-    held = [pltpu.with_memory_space_constraint(x, pltpu.HBM) for x in (therm, noise, drift, noisem)]
-    q, therm, noise, drift, noisem = call(
+    held = [pltpu.with_memory_space_constraint(x, pltpu.HBM) for x in (therm, noise, drift, noisem, neighbours)]
+    q, therm, noise, coef, rows, words = call(
         kick_body,
-        [struct(48, ATOMS + LANES), struct(48, 8, ATOMS), struct(54, 8, ATOMS), struct(144, 9), struct(144, 9)],
-        held, specs=[HBM] * 4,
-        scratch=[pltpu.SemaphoreType.DMA((2, TILES)), pltpu.SemaphoreType.DMA((2,))], flops=4000000, nbytes=3600000,
+        [
+            struct(48, ATOMS + LANES), struct(48, 8, ATOMS), struct(54, 8, ATOMS), struct(288, 8, LANES),
+            struct(TILES, SLOTS, LANES, dtype=I32), struct(SLOTS, LANES, dtype=I32),
+        ],
+        held, specs=[HBM] * 5,
+        scratch=[
+            pltpu.VMEM((144, 9), F32), pltpu.VMEM((144, 9), F32), pltpu.VMEM((SLOTS, ATOMS), I32),
+            pltpu.SemaphoreType.DMA((2, TILES)), pltpu.SemaphoreType.DMA((3,)),
+        ],
+        flops=4000000, nbytes=3600000,
     )
     other_q = shifted(q, "bead", 1)
     modes, part = call(
         modes_body,
         [struct(3, 2, BEADS, ATOMS), struct(48, 8, LANES)],
-        [leave_up, leave_down, pos, mom, other_pos, other_mom, const, therm, noise, drift, noisem],
-        specs=[SMEM] * 2 + [VMEM] * 9,
+        [leave_up, leave_down, pos, mom, other_pos, other_mom, matrices, therm, noise, coef],
+        specs=[SMEM] * 2 + [VMEM] * 8,
         scratch=[pltpu.VMEM((48, 8, LANES), F32), pltpu.VMEM((54, 8, LANES), F32)],
         flops=8000000, nbytes=4000000,
     )
-    bead_pos, bead_mom, mode_mom, up_buf, down_buf, up_pack, down_pack = call(
+    bead_pos, bead_mom, mode_mom, up_buf, down_buf, up_pack, down_pack, codes = call(
         beads_body,
-        [struct(48, ATOMS)] * 3 + [struct(264, LANES)] * 2 + [struct(8, LANES)] * 2,
-        [leave_up, leave_down, modes, q, other_q, const, part, drift, ghost_up, ghost_down],
-        specs=[SMEM] * 2 + [VMEM] * 8,
+        [struct(48, ATOMS)] * 3 + [struct(264, LANES)] * 2 + [struct(8, LANES)] * 2 + [struct(8, LANES, dtype=I32)],
+        [leave_up, leave_down, modes, q, other_q, matrices, tables, part, coef, ghost_up, ghost_down],
+        specs=[SMEM] * 2 + [VMEM] * 9,
         scratch=[pltpu.VMEM((6, 8, LANES), F32)],
         flops=8000000, nbytes=2000000,
     )
     low = shifted(up_buf, "space", 1)
     low2 = shifted(up_pack, "space", 2)
-    work = [therm, noise, mode_mom, drift, noisem]
+    work = [therm, noise, mode_mom, coef]
     aux, down_buf, down_pack = call(
         aux_first, [struct(48, 8, ATOMS), struct(264, LANES), struct(8, LANES)], work + [down_buf, down_pack],
-        specs=[VMEM] * 5 + [ANY] * 2, out_specs=[VMEM, ANY, ANY], alias={5: 1, 6: 2}, flops=1000, nbytes=1000,
+        specs=[VMEM] * 4 + [ANY] * 2, out_specs=[VMEM, ANY, ANY], alias={4: 1, 5: 2}, flops=1000, nbytes=1000,
     )
     high = shifted(down_buf, "space", -1)
     high2 = shifted(down_pack, "space", -2)
-    (aux2,) = call(aux_second, [struct(48, 8, ATOMS)], work, flops=16000000, nbytes=5000000)
-    rows, words, codes = call(
-        lists_body,
-        [struct(TILES, SLOTS, LANES, dtype=I32), struct(SLOTS, LANES, dtype=I32), struct(8, LANES, dtype=I32)],
-        [leave_up, leave_down, neighbours], specs=[SMEM, SMEM, VMEM],
-        flops=1000000, nbytes=300000,
-    )
+    (aux,) = call(aux_second, [struct(48, 8, ATOMS)], [aux] + work, alias={0: 0}, flops=16000000, nbytes=5000000)
     moved, slab, out_aux = call(
         force_body,
         [struct(48, ATOMS), struct(48, ATOMS), struct(48, 8, ATOMS)],
-        [words, codes, rows, bead_pos, bead_mom, aux, aux2, up_pack, low, high, low2, high2],
+        [words, codes, rows, bead_pos, bead_mom, aux, up_pack, low, high, low2, high2],
         out_specs=[HBM] * 3,
         scratch=[
-            pltpu.VMEM((2 * TILES, 48, LANES), F32),
+            pltpu.VMEM((WINDOWS, 48, LANES), F32),
             pltpu.VMEM((48, 8, ATOMS), F32),
             pltpu.VMEM((48, ATOMS), F32),
             pltpu.VMEM((48, ATOMS), F32),

time: 44.3 us -> 36 us (0.81); the launches traced: 43.5 us -> 35.9 us
  Pallas kernels: 25.8 us -> 16.7 us
  starting transfers between devices: 8.5 us -> 15.4 us
  waiting for transfers between devices: 8.35 us -> 3.01 us
    pallas_call x7 -> x6, Pallas kernels: 25.8 us -> 16.7 us  [call(): pl.pallas_call(body, out_shape=outs, in_specs=specs or [VMEM] * len(args)...]
    ppermute x7, starting transfers between devices: 8.5 us -> 15.4 us  [shifted(): lax.ppermute(array, axis, [(i, (i + by) % devices) for i in range(devices)])]
    ppermute x7, waiting for transfers between devices: 8.35 us -> 3.01 us  [shifted(): lax.ppermute(array, axis, [(i, (i + by) % devices) for i in range(devices)])]
  transfers between devices with their start and end apart: 7 -> 7, of which waited for: 4 -> 3; matrix products, arithmetic and copies ran while one was open for 0% -> 0% of each run, Pallas kernels for 10% -> 13%
where the time goes in v2:
time: 36 us; the launch traced here: 35.9 us
  Pallas kernels  16.7 us (46%)
  starting transfers between devices  15.4 us (43%)
  waiting for transfers between devices  3.01 us (8%)
  between operations  0.78 us (2%)
    pallas_call x6, Pallas kernels, call(): pl.pallas_call(body, out_shape=outs, in_specs=specs or [VMEM] * len(args)...  16.7 us
    ppermute x7, starting transfers between devices, shifted(): lax.ppermute(array, axis, [(i, (i + by) % devices) for i in range(devices)])  15.4 us
    ppermute x7, waiting for transfers between devices, shifted(): lax.ppermute(array, axis, [(i, (i + by) % devices) for i in range(devices)])  3.01 us
  transfers between devices with their start and end apart: 7, of which 3 were waited for; matrix products, arithmetic and copies ran while one was open for 0% of the time, Pallas kernels for 13%

profile of v2, /device:TPU:0, one launch (start us, length us, event | category | flops | bytes accessed | tf_op | source)
XLA Modules:
  0.0 35.9 jit_solution(4655799586024676658)
XLA Ops:
  0.6 0.0 copy-start
  0.6 0.0 copy-start.1
  0.7 0.0 copy-start.2
  0.7 0.0 copy-start.6
  0.7 0.0 copy-start.7
  0.7 2.7 %shard_map.148 = (f32[48,1152]{1,0:T(8,128)S(1)}, f32[48,8,1024]{2,1,0:T(8,128)S(1)}, f32[54,8,1024]{2,1,0:T(8,128)S(1)}, f32[288,8,128]{2,1,0:T(8,128)S(1)}, s3...) custom-call(f32[48,8,1024]{2,1,0:T(8,128)} %bitcast.32, f32[54,8,1024]{2,1,0:T(8,128)} %bitcast.31, f32[144,9]{1,0:T(8,128)} %bitcast.33, ...), custom_call_target="tpu_custom_call" | custom-call | flops 4000000 | bytes 3600000 | tf_op jit(solution)/shard_map/pallas_call | solution.py:65
  3.4 0.1 collective-permute-start.2
  3.4 0.0 copy-done
  3.5 0.5 %collective-permute-start = (f32[48,1024]{1,0:T(8,128)S(1)}, f32[48,1024]{1,0:T(8,128)S(1)}, u32[]{:S(2)}, u32[]{:S(2)}) collective-permute-start(f32[48,1024]{1,0:T(8,128)S(1)} %bitcast.27), channel_id=1, source_target_pairs={{0,64},{64,0},{1,65},{65,1},{2,66},{66,2},{3,67},{67,3},{4,68},{68... | collective-permute-start | bytes 589832 | tf_op jit(solution)/shard_map/ppermute | solution.py:83
  3.9 0.1 collective-permute-start.1
  4.0 1.1 %collective-permute-done.ppos_ref = f32[48,1024]{1,0:T(8,128)S(1)} collective-permute-done((f32[48,1024]{1,0:T(8,128)S(1)}, f32[48,1024]{1,0:T(8,128)S(1)}, u32[]{:S(2)}, u32[]{:S(2)}) %collective-permute-start) | collective-permute-done | bytes 196640 | tf_op jit(solution)/shard_map/ppermute | solution.py:83
  5.2 0.3 collective-permute-done.1.pmom_ref
  5.5 0.0 copy-done.6
  5.5 0.0 copy-start.3
  5.5 0.0 copy-start.4
  5.5 0.0 copy-start.5
  5.5 2.5 %shard_map.149 = (f32[3,2,32,1024]{3,2,1,0:T(8,128)S(1)}, f32[48,8,128]{2,1,0:T(8,128)S(1)}) custom-call(s32[8]{0:T(128)S(1)} %copy-done.6, s32[8]{0:T(128)S(1)} %copy-done.7, f32[48,1024]{1,0:T(8,128)S(1)} %bitcast.28, f32[48,1024]{1,0:T(8,128)S(1)} %bitcast.30, f32[48,1024]{1,0:T(8,128)S(1)} %collective-permute-done.ppos_ref, ...), custom_call_target="tpu_custom_call" | custom-call | flops 8000000 | bytes 4000000 | tf_op jit(solution)/shard_map/pallas_call | solution.py:65
  8.0 0.0 collective-permute-done.2.pq_ref
  8.0 0.0 copy-done.3
  8.0 0.0 copy-done.4
  8.0 0.0 copy-done.5
  8.1 1.6 %shard_map.150 = (f32[48,1024]{1,0:T(8,128)S(1)}, f32[48,1024]{1,0:T(8,128)S(1)}, f32[48,1024]{1,0:T(8,128)S(1)}, f32[264,128]{1,0:T(8,128)S(1)}, f32[264,128]{1...) custom-call(s32[8]{0:T(128)S(1)} %copy-done.6, s32[8]{0:T(128)S(1)} %copy-done.7, ...), custom_call_target="tpu_custom_call" | custom-call | flops 8000000 | bytes 2000000 | tf_op jit(solution)/shard_map/pallas_call | solution.py:65
  9.7 1.7 %collective-permute-start.3 = (f32[264,128]{1,0:T(8,128)S(1)}, f32[264,128]{1,0:T(8,128)S(1)}, u32[]{:S(2)}, u32[]{:S(2)}) collective-permute-start(f32[264,128]{1,0:T(8,128)S(1)} %get-tuple-element.41), channel_id=1, source_target_pairs={{0,1},{1,2},{2,3},{3,4},{4,5},{5,6},{6,7},{7,8},{8,9},{9,10},{10,1... | collective-permute-start | bytes 405512 | tf_op jit(solution)/shard_map/ppermute | solution.py:83
  11.4 2.0 %shard_map.151 = (f32[48,8,1024]{2,1,0:T(8,128)S(1)}, f32[264,128]{1,0:T(8,128)S(1)}, f32[8,128]{1,0:T(8,128)S(1)}) custom-call(f32[48,8,1024]{2,1,0:T(8,128)S(1)} %get-tuple-element.26.therm_ref, f32[54,8,1024]{2,1,0:T(8,128)S(1)} %get-tuple-element.27.noise_ref, ...), custom_call_target="tpu_custom_call", output_to_operand_aliasing={{1}: (4, {}), {2}: (5, {})} | custom-call | flops 1000 | bytes 1000 | tf_op jit(solution)/shard_map/pallas_call | solution.py:65
  13.4 5.3 %collective-permute-start.4 = (f32[264,128]{1,0:T(8,128)S(1)}, f32[264,128]{1,0:T(8,128)S(1)}, u32[]{:S(2)}, u32[]{:S(2)}) collective-permute-start(f32[264,128]{1,0:T(8,128)S(1)} %get-tuple-element.42), channel_id=1, source_target_pairs={{0,63},{1,0},{2,1},{3,2},{4,3},{5,4},{6,5},{7,6},{8,7},{9,8},{10,9... | collective-permute-start | bytes 405512 | tf_op jit(solution)/shard_map/ppermute | solution.py:83
  18.7 0.0 collective-permute-start.5
  18.7 7.7 %collective-permute-start.6 = (f32[8,128]{1,0:T(8,128)S(1)}, f32[8,128]{1,0:T(8,128)S(1)}, u32[]{:S(2)}, u32[]{:S(2)}) collective-permute-start(f32[8,128]{1,0:T(8,128)S(1)} %get-tuple-element.43), channel_id=1, source_target_pairs={{0,62},{1,63},{2,0},{3,1},{4,2},{5,3},{6,4},{7,5},{8,6},{9,7},{10,... | collective-permute-start | bytes 12296 | tf_op jit(solution)/shard_map/ppermute | solution.py:83
  26.4 1.6 %collective-permute-done.5.low2_ref = f32[8,128]{1,0:T(8,128)S(1)} collective-permute-done((f32[8,128]{1,0:T(8,128)S(1)}, f32[8,128]{1,0:T(8,128)S(1)}, u32[]{:S(2)}, u32[]{:S(2)}) %collective-permute-start.5) | collective-permute-done | bytes 4128 | tf_op jit(solution)/shard_map/ppermute | solution.py:83
  28.0 0.0 collective-permute-done.6.high2_ref
  28.0 0.0 collective-permute-done.3.low_ref
  28.0 0.0 collective-permute-done.4.high_ref
  28.0 7.9 %shard_map.153 = (f32[48,1024]{1,0:T(8,128)}, f32[48,1024]{1,0:T(8,128)}, f32[48,8,1024]{2,1,0:T(8,128)}) custom-call(s32[32,128]{1,0:T(8,128)S(1)} %get-tuple-element.25.words_vmem, s32[8,128]{1,0:T(8,128)S(1)} %get-tuple-element.32.codes, s32[8,32,128]{2,1,0:T(8,128)S(1)} %get-tuple-element.33.nbr_ref, f32[48,1024]{1,0:T(8,128)S(1)} %get-tuple-element.34.pos_ref, ...), custom_call_target="tpu_custom_call" | custom-call | flops 30000000 | bytes 4000000 | tf_op jit(solution)/shard_map/pallas_call | solution.py:65
  (4 shorter events, 0.0 us)
Async XLA Ops:
  0.6 2.8 %copy-start = (f32[16,3,1024]{2,0,1:T(8,128)S(1)}, f32[16,3,1024]{2,0,1:T(8,128)}, u32[]{:S(2)}) copy-start(f32[16,3,1024]{2,0,1:T(8,128)} %param.13) | copy-start | bytes 589828
  0.6 3.3 %copy-start.1 = (f32[16,3,1024]{2,0,1:T(8,128)S(1)}, f32[16,3,1024]{2,0,1:T(8,128)}, u32[]{:S(2)}) copy-start(f32[16,3,1024]{2,0,1:T(8,128)} %param.14) | copy-start | bytes 589828
  0.7 4.8 %copy-start.2 = (bf16[2,48,96]{2,1,0:T(8,128)(2,1)S(1)}, bf16[2,48,96]{2,1,0:T(8,128)(2,1)}, u32[]{:S(2)}) copy-start(bf16[2,48,96]{2,1,0:T(8,128)(2,1)} %constant.4.clone.const_ref) | copy-start | bytes 55300
  0.7 4.8 %copy-start.6 = (s32[8]{0:T(128)S(1)}, s32[8]{0:T(128)}, u32[]{:S(2)}) copy-start(s32[8]{0:T(128)} %up_ref.3) | copy-start | bytes 100
  0.7 4.8 %copy-start.7 = (s32[8]{0:T(128)S(1)}, s32[8]{0:T(128)}, u32[]{:S(2)}) copy-start(s32[8]{0:T(128)} %down_ref.3) | copy-start | bytes 100
  3.4 4.7 %collective-permute-start.2 = (f32[48,1152]{1,0:T(8,128)S(1)}, f32[48,1152]{1,0:T(8,128)S(1)}, u32[]{:S(2)}, u32[]{:S(2)}) collective-permute-start(f32[48,1152]{1,0:T(8,128)S(1)} %get-tuple-element.30.q_ref), channel_id=1, source_target_pairs={{0,64},{64,0},{1,65},{65,1},{2,66},{66,2},{3,67},{67,3},{4,68},{68... | collective-permute-start | bytes 663560 | tf_op jit(solution)/shard_map/ppermute | solution.py:83
  3.5 1.7 %collective-permute-start = (f32[48,1024]{1,0:T(8,128)S(1)}, f32[48,1024]{1,0:T(8,128)S(1)}, u32[]{:S(2)}, u32[]{:S(2)}) collective-permute-start(f32[48,1024]{1,0:T(8,128)S(1)} %bitcast.27), channel_id=1, source_target_pairs={{0,64},{64,0},{1,65},{65,1},{2,66},{66,2},{3,67},{67,3},{4,68},{68... | collective-permute-start | bytes 589832 | tf_op jit(solution)/shard_map/ppermute | solution.py:83
  3.9 1.5 %collective-permute-start.1 = (f32[48,1024]{1,0:T(8,128)S(1)}, f32[48,1024]{1,0:T(8,128)S(1)}, u32[]{:S(2)}, u32[]{:S(2)}) collective-permute-start(f32[48,1024]{1,0:T(8,128)S(1)} %bitcast.29), channel_id=1, source_target_pairs={{0,64},{64,0},{1,65},{65,1},{2,66},{66,2},{3,67},{67,3},{4,68},{68... | collective-permute-start | bytes 589832 | tf_op jit(solution)/shard_map/ppermute | solution.py:83
  5.5 2.5 %copy-start.3 = (f32[2,32,8]{2,1,0:T(8,128)S(1)}, f32[2,32,8]{2,1,0:T(8,128)}, u32[]{:S(2)}) copy-start(f32[2,32,8]{2,1,0:T(8,128)} %constant.5.clone.table_ref) | copy-start | bytes 6148
  5.5 2.5 %copy-start.4 = (s32[512]{0:T(512)S(1)}, s32[512]{0:T(512)}, u32[]{:S(2)}) copy-start(s32[512]{0:T(512)} %gup_ref.1) | copy-start | bytes 6148
  5.5 2.5 %copy-start.5 = (s32[512]{0:T(512)S(1)}, s32[512]{0:T(512)}, u32[]{:S(2)}) copy-start(s32[512]{0:T(512)} %gdown_ref.1) | copy-start | bytes 6148
  9.7 18.3 %collective-permute-start.3 = (f32[264,128]{1,0:T(8,128)S(1)}, f32[264,128]{1,0:T(8,128)S(1)}, u32[]{:S(2)}, u32[]{:S(2)}) collective-permute-start(f32[264,128]{1,0:T(8,128)S(1)} %get-tuple-element.41), channel_id=1, source_target_pairs={{0,1},{1,2},{2,3},{3,4},{4,5},{5,6},{6,7},{7,8},{8,9},{9,10},{10,1... | collective-permute-start | bytes 405512 | tf_op jit(solution)/shard_map/ppermute | solution.py:83
  13.4 14.6 %collective-permute-start.4 = (f32[264,128]{1,0:T(8,128)S(1)}, f32[264,128]{1,0:T(8,128)S(1)}, u32[]{:S(2)}, u32[]{:S(2)}) collective-permute-start(f32[264,128]{1,0:T(8,128)S(1)} %get-tuple-element.42), channel_id=1, source_target_pairs={{0,63},{1,0},{2,1},{3,2},{4,3},{5,4},{6,5},{7,6},{8,7},{9,8},{10,9... | collective-permute-start | bytes 405512 | tf_op jit(solution)/shard_map/ppermute | solution.py:83
  18.7 9.3 %collective-permute-start.5 = (f32[8,128]{1,0:T(8,128)S(1)}, f32[8,128]{1,0:T(8,128)S(1)}, u32[]{:S(2)}, u32[]{:S(2)}) collective-permute-start(f32[8,128]{1,0:T(8,128)S(1)} %get-tuple-element.40.pack_ref), channel_id=1, source_target_pairs={{0,2},{1,3},{2,4},{3,5},{4,6},{5,7},{6,8},{7,9},{8,10},{9,11},{10,... | collective-permute-start | bytes 12296 | tf_op jit(solution)/shard_map/ppermute | solution.py:83
  18.7 9.3 %collective-permute-start.6 = (f32[8,128]{1,0:T(8,128)S(1)}, f32[8,128]{1,0:T(8,128)S(1)}, u32[]{:S(2)}, u32[]{:S(2)}) collective-permute-start(f32[8,128]{1,0:T(8,128)S(1)} %get-tuple-element.43), channel_id=1, source_target_pairs={{0,62},{1,63},{2,0},{3,1},{4,2},{5,3},{6,4},{7,5},{8,6},{9,7},{10,... | collective-permute-start | bytes 12296 | tf_op jit(solution)/shard_map/ppermute | solution.py:83

commit v3 on v2

--- a/solution.py
+++ b/solution.py
@@ -173,11 +173,11 @@
 
 def kick_body(therm_hbm, noise_hbm, drift_hbm, noisem_hbm, nbr_hbm, q_ref, therm_ref, noise_ref, coef_ref, rows_ref,
               words_ref, drift_ref, noisem_ref, nbr_ref, sems, small):
-    def copies(tile):
-        at = cols(tile)
+    def copies(pair):
+        at = pl.ds(pl.multiple_of(pair * 2 * LANES, 2 * LANES), 2 * LANES)
         return (
-            pltpu.make_async_copy(therm_hbm.at[:, :, at], therm_ref.at[:, :, at], sems.at[0, tile]),
-            pltpu.make_async_copy(noise_hbm.at[:, :, at], noise_ref.at[:, :, at], sems.at[1, tile]),
+            pltpu.make_async_copy(therm_hbm.at[:, :, at], therm_ref.at[:, :, at], sems.at[0, pair]),
+            pltpu.make_async_copy(noise_hbm.at[:, :, at], noise_ref.at[:, :, at], sems.at[1, pair]),
         )
 
     matrices = (
@@ -193,7 +193,7 @@
             copy.start()
         return carry
 
-    lax.fori_loop(0, TILES, begin, 0)
+    lax.fori_loop(0, TILES // 2, begin, 0)
     for copy in matrices:
         copy.wait()
     make_lists(nbr_ref, rows_ref, words_ref)
@@ -216,8 +216,12 @@
 
     def tile_step(tile, carry):
         at = cols(tile)
-        for copy in copies(tile):
-            copy.wait()
+
+        @pl.when((tile & 1) == 0)
+        def _():
+            for copy in copies(lax.shift_right_logical(tile, 1)):
+                copy.wait()
+
         for c in range(3):
             for g in range(2):
                 v = [therm_ref[(g * 8 + k) * 3 + c, :, at] * dcol[g * 8 + k] for k in range(8)]
@@ -259,8 +263,10 @@
         ncol[g] = pick(lambda t: noise_ref[g, :, cols(t)], high, low)
         return carry
 
-    lax.fori_loop(0, 48, therm_step, 0, unroll=12)
-    lax.fori_loop(0, 54, noise_step, 0, unroll=18)
+    for g in range(48):
+        therm_step(g, 0)
+    for g in range(54):
+        noise_step(g, 0)
     for k in range(HALF):
         for c in range(3):
             total = None
@@ -361,32 +367,34 @@
 
 
 def force_body(words_vmem, codes, nbr_ref, pos_ref, mom_ref, aux_ref, pack_ref, low_ref, high_ref,
-               low2_ref, high2_ref, moved_hbm, momout_hbm, auxout_hbm, table, aux, moved_ref, momout_ref, words_ref,
+               low2_ref, high2_ref, moved_hbm, momout_hbm, auxout_hbm, table, aux, moved_ref, momout_ref, came_ref, words_ref,
                sems, tile_sems):
     fetch = pltpu.make_async_copy(words_vmem, words_ref, sems.at[0])
     fetch.start()
     lane = lax.broadcasted_iota(I32, (8, LANES), 1)
     from_low = (lane & 15) < 8
-    packed = [
-        jnp.where(from_low, low_ref[192 + at * 8:200 + at * 8, :], high_ref[192 + at * 8:200 + at * 8, :])
-        for at in range(8)
-    ]
+
+    def turned(value, place):
+        return pltpu.roll(value, LANES - 16 * place, axis=1) if place else value
+
+    for at in range(8):
+        r = slice(192 + at * 8, 200 + at * 8)
+        packed = jnp.where(from_low, low_ref[r, :], high_ref[r, :])
+        for place in range(8 if at < 7 else 4):
+            came_ref[at * 8 + place] = turned(packed, place)
 
     def own_tile(tile, carry):
         at = cols(tile)
         mine = spread(codes[pl.ds(tile, 1), :])
         comes, base = mine >= 0, jnp.maximum(mine, 0)
-        lanes = [base + 16 * m for m in range(8)]
         for g in range(6):
             r = slice(g * 8, g * 8 + 8)
-            new = jnp.where(comes, take(packed[0], lanes[g]), pos_ref[r, at])
+            new = jnp.where(comes, take(came_ref[g], base), pos_ref[r, at])
             table[2 * tile, r, :] = new
             moved_ref[r, at] = new
-            place = 6 + g
-            momout_ref[r, at] = jnp.where(comes, take(packed[place // 8], lanes[place % 8]), mom_ref[r, at])
+            momout_ref[r, at] = jnp.where(comes, take(came_ref[6 + g], base), mom_ref[r, at])
         for g in range(48):
-            place = 12 + g
-            aux[g, :, at] = jnp.where(comes, take(packed[place // 8], lanes[place % 8]), aux_ref[g, :, at])
+            aux[g, :, at] = jnp.where(comes, take(came_ref[12 + g], base), aux_ref[g, :, at])
         return carry
 
     lax.fori_loop(0, TILES, own_tile, 0, unroll=2)
@@ -401,6 +409,7 @@
         (low_ref, jnp.where(from_low, low2_ref[...], pack_ref[...])),
         (high_ref, jnp.where(from_low, pack_ref[...], high2_ref[...])),
     )):
+        sources = [turned(source, g) for g in range(6)]
         for tile in range(GHOST_TILES):
             row = 256 + tile
             mine = spread(buf[row:row + 1, :]).astype(I32)
@@ -408,7 +417,7 @@
             for g in range(6):
                 r = slice(g * 8, g * 8 + 8)
                 old = buf[tile * 48 + g * 8:tile * 48 + g * 8 + 8, :]
-                table[2 * (TILES + side * GHOST_TILES + tile), r, :] = jnp.where(comes, take(source, base + 16 * g), old)
+                table[2 * (TILES + side * GHOST_TILES + tile), r, :] = jnp.where(comes, take(sources[g], base), old)
 
     for g in range(6):
         r = slice(g * 8, g * 8 + 8)
@@ -548,6 +557,7 @@
             pltpu.VMEM((48, 8, ATOMS), F32),
             pltpu.VMEM((48, ATOMS), F32),
             pltpu.VMEM((48, ATOMS), F32),
+            pltpu.VMEM((60, 8, LANES), F32),
             pltpu.SMEM((SLOTS, LANES), I32),
             pltpu.SemaphoreType.DMA((3,)),
             pltpu.SemaphoreType.DMA((TILES,)),

time: 36 us -> 34.5 us (0.958)
  Pallas kernels: 16.7 us -> 15.2 us
    pallas_call x6, Pallas kernels: 16.7 us -> 15.2 us  [call(): pl.pallas_call(body, out_shape=outs, in_specs=specs or [VMEM] * len(args)...]
  transfers between devices with their start and end apart: 7 -> 7, of which waited for: 3 -> 3; matrix products, arithmetic and copies ran while one was open for 0% -> 0% of each run, Pallas kernels for 13% -> 11%
where the time goes in v3:
time: 34.5 us; the launch traced here: 34.4 us
  starting transfers between devices  15.4 us (45%)
  Pallas kernels  15.2 us (44%)
  waiting for transfers between devices  3.01 us (9%)
  between operations  0.79 us (2%)
    ppermute x7, starting transfers between devices, shifted(): lax.ppermute(array, axis, [(i, (i + by) % devices) for i in range(devices)])  15.4 us
    pallas_call x6, Pallas kernels, call(): pl.pallas_call(body, out_shape=outs, in_specs=specs or [VMEM] * len(args)...  15.2 us
    ppermute x7, waiting for transfers between devices, shifted(): lax.ppermute(array, axis, [(i, (i + by) % devices) for i in range(devices)])  3.01 us
  transfers between devices with their start and end apart: 7, of which 3 were waited for; matrix products, arithmetic and copies ran while one was open for 0% of the time, Pallas kernels for 11%

profile of v3, /device:TPU:0, one launch (start us, length us, event | category | flops | bytes accessed | tf_op | source)
XLA Modules:
  0.0 34.4 jit_solution(16072716569476776663)
XLA Ops:
  0.6 0.0 copy-start
  0.6 0.0 copy-start.1
  0.7 0.0 copy-start.2
  0.7 0.0 copy-start.6
  0.7 0.0 copy-start.7
  0.7 2.6 %shard_map.148 = (f32[48,1152]{1,0:T(8,128)S(1)}, f32[48,8,1024]{2,1,0:T(8,128)S(1)}, f32[54,8,1024]{2,1,0:T(8,128)S(1)}, f32[288,8,128]{2,1,0:T(8,128)S(1)}, s3...) custom-call(f32[48,8,1024]{2,1,0:T(8,128)} %bitcast.32, f32[54,8,1024]{2,1,0:T(8,128)} %bitcast.31, f32[144,9]{1,0:T(8,128)} %bitcast.33, ...), custom_call_target="tpu_custom_call" | custom-call | flops 4000000 | bytes 3600000 | tf_op jit(solution)/shard_map/pallas_call | solution.py:65
  3.3 0.1 collective-permute-start.2
  3.4 0.0 copy-done
  3.4 0.5 %collective-permute-start = (f32[48,1024]{1,0:T(8,128)S(1)}, f32[48,1024]{1,0:T(8,128)S(1)}, u32[]{:S(2)}, u32[]{:S(2)}) collective-permute-start(f32[48,1024]{1,0:T(8,128)S(1)} %bitcast.27), channel_id=1, source_target_pairs={{0,64},{64,0},{1,65},{65,1},{2,66},{66,2},{3,67},{67,3},{4,68},{68... | collective-permute-start | bytes 589832 | tf_op jit(solution)/shard_map/ppermute | solution.py:83
  3.9 0.0 copy-done.1
  3.9 0.1 collective-permute-start.1
  4.0 1.1 %collective-permute-done.ppos_ref = f32[48,1024]{1,0:T(8,128)S(1)} collective-permute-done((f32[48,1024]{1,0:T(8,128)S(1)}, f32[48,1024]{1,0:T(8,128)S(1)}, u32[]{:S(2)}, u32[]{:S(2)}) %collective-permute-start) | collective-permute-done | bytes 196640 | tf_op jit(solution)/shard_map/ppermute | solution.py:83
  5.2 0.3 collective-permute-done.1.pmom_ref
  5.5 0.0 copy-done.2
  5.5 0.0 copy-done.6
  5.5 0.0 copy-done.7
  5.5 0.0 copy-start.3
  5.5 0.0 copy-start.4
  5.5 0.0 copy-start.5
  5.5 1.7 %shard_map.149 = (f32[3,2,32,1024]{3,2,1,0:T(8,128)S(1)}, f32[48,8,128]{2,1,0:T(8,128)S(1)}) custom-call(s32[8]{0:T(128)S(1)} %copy-done.6, s32[8]{0:T(128)S(1)} %copy-done.7, f32[48,1024]{1,0:T(8,128)S(1)} %bitcast.28, f32[48,1024]{1,0:T(8,128)S(1)} %bitcast.30, f32[48,1024]{1,0:T(8,128)S(1)} %collective-permute-done.ppos_ref, ...), custom_call_target="tpu_custom_call" | custom-call | flops 8000000 | bytes 4000000 | tf_op jit(solution)/shard_map/pallas_call | solution.py:65
  7.2 0.0 collective-permute-done.2.pq_ref
  7.2 1.6 %shard_map.150 = (f32[48,1024]{1,0:T(8,128)S(1)}, f32[48,1024]{1,0:T(8,128)S(1)}, f32[48,1024]{1,0:T(8,128)S(1)}, f32[264,128]{1,0:T(8,128)S(1)}, f32[264,128]{1...) custom-call(s32[8]{0:T(128)S(1)} %copy-done.6, s32[8]{0:T(128)S(1)} %copy-done.7, ...), custom_call_target="tpu_custom_call" | custom-call | flops 8000000 | bytes 2000000 | tf_op jit(solution)/shard_map/pallas_call | solution.py:65
  8.8 1.7 %collective-permute-start.3 = (f32[264,128]{1,0:T(8,128)S(1)}, f32[264,128]{1,0:T(8,128)S(1)}, u32[]{:S(2)}, u32[]{:S(2)}) collective-permute-start(f32[264,128]{1,0:T(8,128)S(1)} %get-tuple-element.41), channel_id=1, source_target_pairs={{0,1},{1,2},{2,3},{3,4},{4,5},{5,6},{6,7},{7,8},{8,9},{9,10},{10,1... | collective-permute-start | bytes 405512 | tf_op jit(solution)/shard_map/ppermute | solution.py:83
  10.5 2.0 %shard_map.151 = (f32[48,8,1024]{2,1,0:T(8,128)S(1)}, f32[264,128]{1,0:T(8,128)S(1)}, f32[8,128]{1,0:T(8,128)S(1)}) custom-call(f32[48,8,1024]{2,1,0:T(8,128)S(1)} %get-tuple-element.26.therm_ref, f32[54,8,1024]{2,1,0:T(8,128)S(1)} %get-tuple-element.27.noise_ref, ...), custom_call_target="tpu_custom_call", output_to_operand_aliasing={{1}: (4, {}), {2}: (5, {})} | custom-call | flops 1000 | bytes 1000 | tf_op jit(solution)/shard_map/pallas_call | solution.py:65
  12.5 5.3 %collective-permute-start.4 = (f32[264,128]{1,0:T(8,128)S(1)}, f32[264,128]{1,0:T(8,128)S(1)}, u32[]{:S(2)}, u32[]{:S(2)}) collective-permute-start(f32[264,128]{1,0:T(8,128)S(1)} %get-tuple-element.42), channel_id=1, source_target_pairs={{0,63},{1,0},{2,1},{3,2},{4,3},{5,4},{6,5},{7,6},{8,7},{9,8},{10,9... | collective-permute-start | bytes 405512 | tf_op jit(solution)/shard_map/ppermute | solution.py:83
  17.8 0.0 collective-permute-start.5
  17.8 7.7 %collective-permute-start.6 = (f32[8,128]{1,0:T(8,128)S(1)}, f32[8,128]{1,0:T(8,128)S(1)}, u32[]{:S(2)}, u32[]{:S(2)}) collective-permute-start(f32[8,128]{1,0:T(8,128)S(1)} %get-tuple-element.43), channel_id=1, source_target_pairs={{0,62},{1,63},{2,0},{3,1},{4,2},{5,3},{6,4},{7,5},{8,6},{9,7},{10,... | collective-permute-start | bytes 12296 | tf_op jit(solution)/shard_map/ppermute | solution.py:83
  25.6 1.6 %collective-permute-done.5.low2_ref = f32[8,128]{1,0:T(8,128)S(1)} collective-permute-done((f32[8,128]{1,0:T(8,128)S(1)}, f32[8,128]{1,0:T(8,128)S(1)}, u32[]{:S(2)}, u32[]{:S(2)}) %collective-permute-start.5) | collective-permute-done | bytes 4128 | tf_op jit(solution)/shard_map/ppermute | solution.py:83
  27.1 0.0 collective-permute-done.6.high2_ref
  27.1 0.0 collective-permute-done.3.low_ref
  27.1 0.0 collective-permute-done.4.high_ref
  27.1 7.2 %shard_map.153 = (f32[48,1024]{1,0:T(8,128)}, f32[48,1024]{1,0:T(8,128)}, f32[48,8,1024]{2,1,0:T(8,128)}) custom-call(s32[32,128]{1,0:T(8,128)S(1)} %get-tuple-element.25.words_vmem, s32[8,128]{1,0:T(8,128)S(1)} %get-tuple-element.32.codes, s32[8,32,128]{2,1,0:T(8,128)S(1)} %get-tuple-element.33.nbr_ref, f32[48,1024]{1,0:T(8,128)S(1)} %get-tuple-element.34.pos_ref, ...), custom_call_target="tpu_custom_call" | custom-call | flops 30000000 | bytes 4000000 | tf_op jit(solution)/shard_map/pallas_call | solution.py:65
  (4 shorter events, 0.0 us)
Async XLA Ops:
  0.6 2.8 %copy-start = (f32[16,3,1024]{2,0,1:T(8,128)S(1)}, f32[16,3,1024]{2,0,1:T(8,128)}, u32[]{:S(2)}) copy-start(f32[16,3,1024]{2,0,1:T(8,128)} %param.13) | copy-start | bytes 589828
  0.6 3.3 %copy-start.1 = (f32[16,3,1024]{2,0,1:T(8,128)S(1)}, f32[16,3,1024]{2,0,1:T(8,128)}, u32[]{:S(2)}) copy-start(f32[16,3,1024]{2,0,1:T(8,128)} %param.14) | copy-start | bytes 589828
  0.7 4.8 %copy-start.2 = (bf16[2,48,96]{2,1,0:T(8,128)(2,1)S(1)}, bf16[2,48,96]{2,1,0:T(8,128)(2,1)}, u32[]{:S(2)}) copy-start(bf16[2,48,96]{2,1,0:T(8,128)(2,1)} %constant.4.clone.const_ref) | copy-start | bytes 55300
  0.7 4.8 %copy-start.6 = (s32[8]{0:T(128)S(1)}, s32[8]{0:T(128)}, u32[]{:S(2)}) copy-start(s32[8]{0:T(128)} %up_ref.3) | copy-start | bytes 100
  0.7 4.8 %copy-start.7 = (s32[8]{0:T(128)S(1)}, s32[8]{0:T(128)}, u32[]{:S(2)}) copy-start(s32[8]{0:T(128)} %down_ref.3) | copy-start | bytes 100
  3.3 3.8 %collective-permute-start.2 = (f32[48,1152]{1,0:T(8,128)S(1)}, f32[48,1152]{1,0:T(8,128)S(1)}, u32[]{:S(2)}, u32[]{:S(2)}) collective-permute-start(f32[48,1152]{1,0:T(8,128)S(1)} %get-tuple-element.30.q_ref), channel_id=1, source_target_pairs={{0,64},{64,0},{1,65},{65,1},{2,66},{66,2},{3,67},{67,3},{4,68},{68... | collective-permute-start | bytes 663560 | tf_op jit(solution)/shard_map/ppermute | solution.py:83
  3.4 1.7 %collective-permute-start = (f32[48,1024]{1,0:T(8,128)S(1)}, f32[48,1024]{1,0:T(8,128)S(1)}, u32[]{:S(2)}, u32[]{:S(2)}) collective-permute-start(f32[48,1024]{1,0:T(8,128)S(1)} %bitcast.27), channel_id=1, source_target_pairs={{0,64},{64,0},{1,65},{65,1},{2,66},{66,2},{3,67},{67,3},{4,68},{68... | collective-permute-start | bytes 589832 | tf_op jit(solution)/shard_map/ppermute | solution.py:83
  3.9 1.5 %collective-permute-start.1 = (f32[48,1024]{1,0:T(8,128)S(1)}, f32[48,1024]{1,0:T(8,128)S(1)}, u32[]{:S(2)}, u32[]{:S(2)}) collective-permute-start(f32[48,1024]{1,0:T(8,128)S(1)} %bitcast.29), channel_id=1, source_target_pairs={{0,64},{64,0},{1,65},{65,1},{2,66},{66,2},{3,67},{67,3},{4,68},{68... | collective-permute-start | bytes 589832 | tf_op jit(solution)/shard_map/ppermute | solution.py:83
  5.5 1.7 %copy-start.3 = (f32[2,32,8]{2,1,0:T(8,128)S(1)}, f32[2,32,8]{2,1,0:T(8,128)}, u32[]{:S(2)}) copy-start(f32[2,32,8]{2,1,0:T(8,128)} %constant.5.clone.table_ref) | copy-start | bytes 6148
  5.5 1.7 %copy-start.4 = (s32[512]{0:T(512)S(1)}, s32[512]{0:T(512)}, u32[]{:S(2)}) copy-start(s32[512]{0:T(512)} %gup_ref.1) | copy-start | bytes 6148
  5.5 1.7 %copy-start.5 = (s32[512]{0:T(512)S(1)}, s32[512]{0:T(512)}, u32[]{:S(2)}) copy-start(s32[512]{0:T(512)} %gdown_ref.1) | copy-start | bytes 6148
  8.8 18.3 %collective-permute-start.3 = (f32[264,128]{1,0:T(8,128)S(1)}, f32[264,128]{1,0:T(8,128)S(1)}, u32[]{:S(2)}, u32[]{:S(2)}) collective-permute-start(f32[264,128]{1,0:T(8,128)S(1)} %get-tuple-element.41), channel_id=1, source_target_pairs={{0,1},{1,2},{2,3},{3,4},{4,5},{5,6},{6,7},{7,8},{8,9},{9,10},{10,1... | collective-permute-start | bytes 405512 | tf_op jit(solution)/shard_map/ppermute | solution.py:83
  12.5 14.6 %collective-permute-start.4 = (f32[264,128]{1,0:T(8,128)S(1)}, f32[264,128]{1,0:T(8,128)S(1)}, u32[]{:S(2)}, u32[]{:S(2)}) collective-permute-start(f32[264,128]{1,0:T(8,128)S(1)} %get-tuple-element.42), channel_id=1, source_target_pairs={{0,63},{1,0},{2,1},{3,2},{4,3},{5,4},{6,5},{7,6},{8,7},{9,8},{10,9... | collective-permute-start | bytes 405512 | tf_op jit(solution)/shard_map/ppermute | solution.py:83
  17.8 9.3 %collective-permute-start.5 = (f32[8,128]{1,0:T(8,128)S(1)}, f32[8,128]{1,0:T(8,128)S(1)}, u32[]{:S(2)}, u32[]{:S(2)}) collective-permute-start(f32[8,128]{1,0:T(8,128)S(1)} %get-tuple-element.40.pack_ref), channel_id=1, source_target_pairs={{0,2},{1,3},{2,4},{3,5},{4,6},{5,7},{6,8},{7,9},{8,10},{9,11},{10,... | collective-permute-start | bytes 12296 | tf_op jit(solution)/shard_map/ppermute | solution.py:83
  17.8 9.3 %collective-permute-start.6 = (f32[8,128]{1,0:T(8,128)S(1)}, f32[8,128]{1,0:T(8,128)S(1)}, u32[]{:S(2)}, u32[]{:S(2)}) collective-permute-start(f32[8,128]{1,0:T(8,128)S(1)} %get-tuple-element.43), channel_id=1, source_target_pairs={{0,62},{1,63},{2,0},{3,1},{4,2},{5,3},{6,4},{7,5},{8,6},{9,7},{10,... | collective-permute-start | bytes 12296 | tf_op jit(solution)/shard_map/ppermute | solution.py:83

commit v4 on v3

--- a/solution.py
+++ b/solution.py
@@ -437,11 +437,13 @@
         def pull(found, hit, low, place):
             return [jnp.where(hit, take(table[place, g * 8:g * 8 + 8, :], low), found[g]) for g in range(6)]
 
-        def push(total, found):
+        def push(total, found, valid=None):
             done = list(total)
             for half in range(2):
                 d = [own[2 * c + half] - found[2 * c + half] for c in range(3)]
-                weight = jnp.exp((d[0] * d[0] + d[1] * d[1] + d[2] * d[2]) * (-0.5 / core_width))
+                weight = jnp.exp2((d[0] * d[0] + d[1] * d[1] + d[2] * d[2]) * (-0.5 / core_width / math.log(2.0)))
+                if valid is not None:
+                    weight = jnp.where(valid, weight, 0.0)
                 for c in range(3):
                     done[2 * c + half] = done[2 * c + half] + d[c] * weight
             return tuple(done)
@@ -458,8 +460,9 @@
                     index = spread(nbr_ref[tile, pl.ds(first + u, 1), :])
                     high, low = lax.shift_right_logical(index, 7), index & 127
                     place = words[u] & 31
-                    found = pull(own, high == 0, low, place)
-                    total = push(total, pull(found, high == 1, low, (place + 2) & 31))
+                    after = (place + 2) & 31
+                    found = [take(table[place, g * 8:g * 8 + 8, :], low) for g in range(6)]
+                    total = push(total, pull(found, high == 1, low, after), high < 2)
                 return total
 
             def slow(total):

time: 34.5 us -> 34.4 us (level)
  no operation moved by 1% of the time
where the time goes in v4:
time: 34.4 us; the launch traced here: 34.3 us
  starting transfers between devices  15.4 us (45%)
  Pallas kernels  15.1 us (44%)
  waiting for transfers between devices  3.01 us (9%)
  between operations  0.79 us (2%)
    ppermute x7, starting transfers between devices, shifted(): lax.ppermute(array, axis, [(i, (i + by) % devices) for i in range(devices)])  15.4 us
    pallas_call x6, Pallas kernels, call(): pl.pallas_call(body, out_shape=outs, in_specs=specs or [VMEM] * len(args)...  15.1 us
    ppermute x7, waiting for transfers between devices, shifted(): lax.ppermute(array, axis, [(i, (i + by) % devices) for i in range(devices)])  3.01 us
  transfers between devices with their start and end apart: 7, of which 3 were waited for; matrix products, arithmetic and copies ran while one was open for 0% of the time, Pallas kernels for 11%

profile of v4, /device:TPU:0, one launch (start us, length us, event | category | flops | bytes accessed | tf_op | source)
XLA Modules:
  0.0 34.3 jit_solution(14244529251347463218)
XLA Ops:
  0.6 0.0 copy-start
  0.6 0.0 copy-start.1
  0.7 0.0 copy-start.2
  0.7 0.0 copy-start.6
  0.7 0.0 copy-start.7
  0.7 2.6 %shard_map.148 = (f32[48,1152]{1,0:T(8,128)S(1)}, f32[48,8,1024]{2,1,0:T(8,128)S(1)}, f32[54,8,1024]{2,1,0:T(8,128)S(1)}, f32[288,8,128]{2,1,0:T(8,128)S(1)}, s3...) custom-call(f32[48,8,1024]{2,1,0:T(8,128)} %bitcast.32, f32[54,8,1024]{2,1,0:T(8,128)} %bitcast.31, f32[144,9]{1,0:T(8,128)} %bitcast.33, ...), custom_call_target="tpu_custom_call" | custom-call | flops 4000000 | bytes 3600000 | tf_op jit(solution)/shard_map/pallas_call | solution.py:65
  3.3 0.1 collective-permute-start.2
  3.4 0.0 copy-done
  3.4 0.5 %collective-permute-start = (f32[48,1024]{1,0:T(8,128)S(1)}, f32[48,1024]{1,0:T(8,128)S(1)}, u32[]{:S(2)}, u32[]{:S(2)}) collective-permute-start(f32[48,1024]{1,0:T(8,128)S(1)} %bitcast.27), channel_id=1, source_target_pairs={{0,64},{64,0},{1,65},{65,1},{2,66},{66,2},{3,67},{67,3},{4,68},{68... | collective-permute-start | bytes 589832 | tf_op jit(solution)/shard_map/ppermute | solution.py:83
  3.9 0.0 copy-done.1
  3.9 0.1 collective-permute-start.1
  4.0 1.1 %collective-permute-done.ppos_ref = f32[48,1024]{1,0:T(8,128)S(1)} collective-permute-done((f32[48,1024]{1,0:T(8,128)S(1)}, f32[48,1024]{1,0:T(8,128)S(1)}, u32[]{:S(2)}, u32[]{:S(2)}) %collective-permute-start) | collective-permute-done | bytes 196640 | tf_op jit(solution)/shard_map/ppermute | solution.py:83
  5.2 0.3 collective-permute-done.1.pmom_ref
  5.5 0.0 copy-done.2
  5.5 0.0 copy-done.6
  5.5 0.0 copy-done.7
  5.5 0.0 copy-start.3
  5.5 0.0 copy-start.4
  5.5 0.0 copy-start.5
  5.5 1.7 %shard_map.149 = (f32[3,2,32,1024]{3,2,1,0:T(8,128)S(1)}, f32[48,8,128]{2,1,0:T(8,128)S(1)}) custom-call(s32[8]{0:T(128)S(1)} %copy-done.6, s32[8]{0:T(128)S(1)} %copy-done.7, f32[48,1024]{1,0:T(8,128)S(1)} %bitcast.28, f32[48,1024]{1,0:T(8,128)S(1)} %bitcast.30, f32[48,1024]{1,0:T(8,128)S(1)} %collective-permute-done.ppos_ref, ...), custom_call_target="tpu_custom_call" | custom-call | flops 8000000 | bytes 4000000 | tf_op jit(solution)/shard_map/pallas_call | solution.py:65
  7.2 0.0 collective-permute-done.2.pq_ref
  7.2 1.6 %shard_map.150 = (f32[48,1024]{1,0:T(8,128)S(1)}, f32[48,1024]{1,0:T(8,128)S(1)}, f32[48,1024]{1,0:T(8,128)S(1)}, f32[264,128]{1,0:T(8,128)S(1)}, f32[264,128]{1...) custom-call(s32[8]{0:T(128)S(1)} %copy-done.6, s32[8]{0:T(128)S(1)} %copy-done.7, ...), custom_call_target="tpu_custom_call" | custom-call | flops 8000000 | bytes 2000000 | tf_op jit(solution)/shard_map/pallas_call | solution.py:65
  8.8 1.7 %collective-permute-start.3 = (f32[264,128]{1,0:T(8,128)S(1)}, f32[264,128]{1,0:T(8,128)S(1)}, u32[]{:S(2)}, u32[]{:S(2)}) collective-permute-start(f32[264,128]{1,0:T(8,128)S(1)} %get-tuple-element.41), channel_id=1, source_target_pairs={{0,1},{1,2},{2,3},{3,4},{4,5},{5,6},{6,7},{7,8},{8,9},{9,10},{10,1... | collective-permute-start | bytes 405512 | tf_op jit(solution)/shard_map/ppermute | solution.py:83
  10.5 2.0 %shard_map.151 = (f32[48,8,1024]{2,1,0:T(8,128)S(1)}, f32[264,128]{1,0:T(8,128)S(1)}, f32[8,128]{1,0:T(8,128)S(1)}) custom-call(f32[48,8,1024]{2,1,0:T(8,128)S(1)} %get-tuple-element.26.therm_ref, f32[54,8,1024]{2,1,0:T(8,128)S(1)} %get-tuple-element.27.noise_ref, ...), custom_call_target="tpu_custom_call", output_to_operand_aliasing={{1}: (4, {}), {2}: (5, {})} | custom-call | flops 1000 | bytes 1000 | tf_op jit(solution)/shard_map/pallas_call | solution.py:65
  12.5 5.3 %collective-permute-start.4 = (f32[264,128]{1,0:T(8,128)S(1)}, f32[264,128]{1,0:T(8,128)S(1)}, u32[]{:S(2)}, u32[]{:S(2)}) collective-permute-start(f32[264,128]{1,0:T(8,128)S(1)} %get-tuple-element.42), channel_id=1, source_target_pairs={{0,63},{1,0},{2,1},{3,2},{4,3},{5,4},{6,5},{7,6},{8,7},{9,8},{10,9... | collective-permute-start | bytes 405512 | tf_op jit(solution)/shard_map/ppermute | solution.py:83
  17.8 0.0 collective-permute-start.5
  17.8 7.7 %collective-permute-start.6 = (f32[8,128]{1,0:T(8,128)S(1)}, f32[8,128]{1,0:T(8,128)S(1)}, u32[]{:S(2)}, u32[]{:S(2)}) collective-permute-start(f32[8,128]{1,0:T(8,128)S(1)} %get-tuple-element.43), channel_id=1, source_target_pairs={{0,62},{1,63},{2,0},{3,1},{4,2},{5,3},{6,4},{7,5},{8,6},{9,7},{10,... | collective-permute-start | bytes 12296 | tf_op jit(solution)/shard_map/ppermute | solution.py:83
  25.6 1.6 %collective-permute-done.5.low2_ref = f32[8,128]{1,0:T(8,128)S(1)} collective-permute-done((f32[8,128]{1,0:T(8,128)S(1)}, f32[8,128]{1,0:T(8,128)S(1)}, u32[]{:S(2)}, u32[]{:S(2)}) %collective-permute-start.5) | collective-permute-done | bytes 4128 | tf_op jit(solution)/shard_map/ppermute | solution.py:83
  27.1 0.0 collective-permute-done.6.high2_ref
  27.1 0.0 collective-permute-done.3.low_ref
  27.1 0.0 collective-permute-done.4.high_ref
  27.1 7.2 %shard_map.153 = (f32[48,1024]{1,0:T(8,128)}, f32[48,1024]{1,0:T(8,128)}, f32[48,8,1024]{2,1,0:T(8,128)}) custom-call(s32[32,128]{1,0:T(8,128)S(1)} %get-tuple-element.25.words_vmem, s32[8,128]{1,0:T(8,128)S(1)} %get-tuple-element.32.codes, s32[8,32,128]{2,1,0:T(8,128)S(1)} %get-tuple-element.33.nbr_ref, f32[48,1024]{1,0:T(8,128)S(1)} %get-tuple-element.34.pos_ref, ...), custom_call_target="tpu_custom_call" | custom-call | flops 30000000 | bytes 4000000 | tf_op jit(solution)/shard_map/pallas_call | solution.py:65
  (4 shorter events, 0.0 us)
Async XLA Ops:
  0.6 2.8 %copy-start = (f32[16,3,1024]{2,0,1:T(8,128)S(1)}, f32[16,3,1024]{2,0,1:T(8,128)}, u32[]{:S(2)}) copy-start(f32[16,3,1024]{2,0,1:T(8,128)} %param.13) | copy-start | bytes 589828
  0.6 3.3 %copy-start.1 = (f32[16,3,1024]{2,0,1:T(8,128)S(1)}, f32[16,3,1024]{2,0,1:T(8,128)}, u32[]{:S(2)}) copy-start(f32[16,3,1024]{2,0,1:T(8,128)} %param.14) | copy-start | bytes 589828
  0.7 4.8 %copy-start.2 = (bf16[2,48,96]{2,1,0:T(8,128)(2,1)S(1)}, bf16[2,48,96]{2,1,0:T(8,128)(2,1)}, u32[]{:S(2)}) copy-start(bf16[2,48,96]{2,1,0:T(8,128)(2,1)} %constant.4.clone.const_ref) | copy-start | bytes 55300
  0.7 4.8 %copy-start.6 = (s32[8]{0:T(128)S(1)}, s32[8]{0:T(128)}, u32[]{:S(2)}) copy-start(s32[8]{0:T(128)} %up_ref.3) | copy-start | bytes 100
  0.7 4.8 %copy-start.7 = (s32[8]{0:T(128)S(1)}, s32[8]{0:T(128)}, u32[]{:S(2)}) copy-start(s32[8]{0:T(128)} %down_ref.3) | copy-start | bytes 100
  3.3 3.8 %collective-permute-start.2 = (f32[48,1152]{1,0:T(8,128)S(1)}, f32[48,1152]{1,0:T(8,128)S(1)}, u32[]{:S(2)}, u32[]{:S(2)}) collective-permute-start(f32[48,1152]{1,0:T(8,128)S(1)} %get-tuple-element.30.q_ref), channel_id=1, source_target_pairs={{0,64},{64,0},{1,65},{65,1},{2,66},{66,2},{3,67},{67,3},{4,68},{68... | collective-permute-start | bytes 663560 | tf_op jit(solution)/shard_map/ppermute | solution.py:83
  3.4 1.7 %collective-permute-start = (f32[48,1024]{1,0:T(8,128)S(1)}, f32[48,1024]{1,0:T(8,128)S(1)}, u32[]{:S(2)}, u32[]{:S(2)}) collective-permute-start(f32[48,1024]{1,0:T(8,128)S(1)} %bitcast.27), channel_id=1, source_target_pairs={{0,64},{64,0},{1,65},{65,1},{2,66},{66,2},{3,67},{67,3},{4,68},{68... | collective-permute-start | bytes 589832 | tf_op jit(solution)/shard_map/ppermute | solution.py:83
  3.9 1.5 %collective-permute-start.1 = (f32[48,1024]{1,0:T(8,128)S(1)}, f32[48,1024]{1,0:T(8,128)S(1)}, u32[]{:S(2)}, u32[]{:S(2)}) collective-permute-start(f32[48,1024]{1,0:T(8,128)S(1)} %bitcast.29), channel_id=1, source_target_pairs={{0,64},{64,0},{1,65},{65,1},{2,66},{66,2},{3,67},{67,3},{4,68},{68... | collective-permute-start | bytes 589832 | tf_op jit(solution)/shard_map/ppermute | solution.py:83
  5.5 1.7 %copy-start.3 = (f32[2,32,8]{2,1,0:T(8,128)S(1)}, f32[2,32,8]{2,1,0:T(8,128)}, u32[]{:S(2)}) copy-start(f32[2,32,8]{2,1,0:T(8,128)} %constant.5.clone.table_ref) | copy-start | bytes 6148
  5.5 1.7 %copy-start.4 = (s32[512]{0:T(512)S(1)}, s32[512]{0:T(512)}, u32[]{:S(2)}) copy-start(s32[512]{0:T(512)} %gup_ref.1) | copy-start | bytes 6148
  5.5 1.7 %copy-start.5 = (s32[512]{0:T(512)S(1)}, s32[512]{0:T(512)}, u32[]{:S(2)}) copy-start(s32[512]{0:T(512)} %gdown_ref.1) | copy-start | bytes 6148
  8.8 18.3 %collective-permute-start.3 = (f32[264,128]{1,0:T(8,128)S(1)}, f32[264,128]{1,0:T(8,128)S(1)}, u32[]{:S(2)}, u32[]{:S(2)}) collective-permute-start(f32[264,128]{1,0:T(8,128)S(1)} %get-tuple-element.41), channel_id=1, source_target_pairs={{0,1},{1,2},{2,3},{3,4},{4,5},{5,6},{6,7},{7,8},{8,9},{9,10},{10,1... | collective-permute-start | bytes 405512 | tf_op jit(solution)/shard_map/ppermute | solution.py:83
  12.5 14.6 %collective-permute-start.4 = (f32[264,128]{1,0:T(8,128)S(1)}, f32[264,128]{1,0:T(8,128)S(1)}, u32[]{:S(2)}, u32[]{:S(2)}) collective-permute-start(f32[264,128]{1,0:T(8,128)S(1)} %get-tuple-element.42), channel_id=1, source_target_pairs={{0,63},{1,0},{2,1},{3,2},{4,3},{5,4},{6,5},{7,6},{8,7},{9,8},{10,9... | collective-permute-start | bytes 405512 | tf_op jit(solution)/shard_map/ppermute | solution.py:83
  17.8 9.3 %collective-permute-start.5 = (f32[8,128]{1,0:T(8,128)S(1)}, f32[8,128]{1,0:T(8,128)S(1)}, u32[]{:S(2)}, u32[]{:S(2)}) collective-permute-start(f32[8,128]{1,0:T(8,128)S(1)} %get-tuple-element.40.pack_ref), channel_id=1, source_target_pairs={{0,2},{1,3},{2,4},{3,5},{4,6},{5,7},{6,8},{7,9},{8,10},{9,11},{10,... | collective-permute-start | bytes 12296 | tf_op jit(solution)/shard_map/ppermute | solution.py:83
  17.8 9.3 %collective-permute-start.6 = (f32[8,128]{1,0:T(8,128)S(1)}, f32[8,128]{1,0:T(8,128)S(1)}, u32[]{:S(2)}, u32[]{:S(2)}) collective-permute-start(f32[8,128]{1,0:T(8,128)S(1)} %get-tuple-element.43), channel_id=1, source_target_pairs={{0,62},{1,63},{2,0},{3,1},{4,2},{5,3},{6,4},{7,5},{8,6},{9,7},{10,... | collective-permute-start | bytes 12296 | tf_op jit(solution)/shard_map/ppermute | solution.py:83
